TPU v7x, 512 devices: a whole 4x4x16 slice. The times are simulated.
512 devices in a mesh: loop: 32 (over z, y_hi), rep: 4 (over x), feat: 4 (over y_lo, core).
Axes of the slice: x: 4, y: 4 (y_hi: 2, y_lo: 2; y = y_hi * 2 + y_lo), z: 16, core: 2. Of those that a mesh axis runs over, the one named last changes fastest.
Arguments:
- features: bfloat16 [128, 32768], P('feat', 'loop'), may hold values from -6 to 6
- tile_values: bfloat16 [32, 4, 112, 128, 128], P('loop', 'rep'), may hold values from -0.1875 to 0.1875
- tile_coords: int32 [32, 4, 2, 112], P('loop', 'rep'), may hold values from 0 to 7, as said below
- section_counts: int32 [32, 4, 8], P('loop', 'rep'), may hold values from 0 to 64, as said below
- weight_one: bfloat16 [128, 128], replicated, may hold values from -0.5 to 0.5
- weight_two: bfloat16 [128, 128], replicated, may hold values from -0.5 to 0.5
- cotangent: bfloat16 [128, 32768], P(None, ('loop', 'feat')), may hold values from -24 to 24
Outputs:
- grad_one: float32 [128, 128], replicated
- grad_two: float32 [128, 128], replicated
- input_grad: bfloat16 [128, 32768], P('feat', 'loop')
Inputs may be any that keep to these rules, and one draw needn't show every extreme that they name: `tile_coords`: slots of a list are grouped by section in order of sections; the live slots of one section name distinct (row, column) pairs; slots past the list's total count hold 0. `section_counts`: section k of rep index r covers the column block r + 4 * k places below the list's own loop index; sections with r + 4 * k of 32 or more hold 0.
All inputs are finite; a program needn't handle non-finite values.
Results may differ from a plain program's by a relative error of at most 0.029.
Values may be sent and summed in bfloat16 or wider, within the bound.
A program may use at most 64 MiB of HBM per device.

v0:
```python
import math

import jax
import jax.numpy as jnp
from jax import lax
from jax.sharding import PartitionSpec as P

tile_batch = 8


def passed_along(value, axis, steps):
    count = lax.axis_size(axis)
    pairs = [(source, (source + steps) % count) for source in range(count)]
    return lax.ppermute(value, axis, pairs)


def silu_slope(argument):
    sigmoid_value = jax.nn.sigmoid(argument)
    return sigmoid_value * (1.0 + argument * (1.0 - sigmoid_value))


def section_term(source, section_id, layout, transposed, enabled=True):
    tile_set, row_ids, col_ids, starts, filled, panels = layout
    feat_width = source.shape[0]
    tile_side = tile_set.shape[-1]
    slot_total = tile_set.shape[0]
    shaped = source.reshape(feat_width, panels, tile_side)
    first = starts[section_id]
    number = jnp.where(enabled, filled[section_id], 0)
    rounds = (number + tile_batch - 1) // tile_batch
    offsets = jnp.arange(tile_batch, dtype=jnp.int32)
    panel_ids = jnp.arange(panels, dtype=jnp.int32)

    def one_round(round_id, running):
        within = round_id * tile_batch + offsets
        alive_mask = within < number
        slot_ids = jnp.minimum(first + within, slot_total - 1)
        chosen = tile_set[slot_ids]
        if transposed:
            picked = shaped[:, row_ids[slot_ids], :]
            products = jnp.einsum(
                "dba,bac->dbc", picked, chosen, preferred_element_type=jnp.float32
            )
            target = col_ids[slot_ids]
        else:
            picked = shaped[:, col_ids[slot_ids], :]
            products = jnp.einsum(
                "dbc,bac->dba", picked, chosen, preferred_element_type=jnp.float32
            )
            target = row_ids[slot_ids]
        placing = ((target[:, None] == panel_ids[None, :]) & alive_mask[:, None]).astype(
            jnp.float32
        )
        return running + jnp.einsum(
            "dbe,bp->dpe", products, placing, precision=lax.Precision.HIGHEST
        )

    zero_block = jnp.zeros((feat_width, panels, tile_side), jnp.float32)
    return lax.fori_loop(0, rounds, one_round, zero_block).reshape(feat_width, panels * tile_side)


def advance(block, stride):
    return passed_along(block, "loop", stride)


def forward_product(source, layout):
    loop_size = lax.axis_size("loop")
    rep_size = lax.axis_size("rep")
    rep_index = lax.axis_index("rep")
    sections = -(-loop_size // rep_size)
    stride = rep_size % loop_size
    current = source
    for bit in range(rep_size.bit_length() - 1):
        jump = (1 << bit) % loop_size
        moved = passed_along(current, "loop", jump)
        current = jnp.where((rep_index >> bit) % 2 == 1, moved, current)
    running = section_term(current, 0, layout, False)

    def onward(step_id, carry):
        ahead, acc = carry
        ahead = advance(ahead, stride)
        return (ahead, acc + section_term(ahead, step_id, layout, False))

    ahead, running = lax.fori_loop(1, sections, onward, (current, running))
    return running


def transposed_product(source, layout):
    loop_size = lax.axis_size("loop")
    rep_size = lax.axis_size("rep")
    rep_index = lax.axis_index("rep")
    sections = -(-loop_size // rep_size)
    stride = rep_size % loop_size
    running = section_term(source, sections - 1, layout, True)

    def backward(step_id, acc):
        acc = passed_along(acc.astype(jnp.bfloat16), "loop", -stride).astype(acc.dtype)
        return acc + section_term(source, sections - 1 - step_id, layout, True)

    running = lax.fori_loop(1, sections, backward, running)
    for bit in range(rep_size.bit_length() - 1):
        jump = (1 << bit) % loop_size
        moved = passed_along(running.astype(jnp.bfloat16), "loop", -jump).astype(running.dtype)
        running = jnp.where((rep_index >> bit) % 2 == 1, moved, running)
    return running


def to_nodes(partial_value):
    summed = lax.psum(partial_value.astype(jnp.bfloat16), "rep")
    return lax.all_to_all(summed, "feat", split_axis=1, concat_axis=0, tiled=True)


def to_features(node_block):
    return lax.all_to_all(node_block, "feat", split_axis=0, concat_axis=1, tiled=True)


def weight_grad(mixed, slope):
    part_sum = jnp.einsum("dq,eq->de", mixed, slope, preferred_element_type=jnp.float32)
    return lax.psum(part_sum, ("loop", "feat"))


def shards(features, tile_values, tile_coords, section_counts, weight_one, weight_two, cotangent):
    tile_set = tile_values[0, 0]
    row_ids = tile_coords[0, 0, 0]
    col_ids = tile_coords[0, 0, 1]
    filled = section_counts[0, 0]
    starts = jnp.cumsum(filled) - filled
    panels = features.shape[1] // tile_set.shape[-1]
    layout = (tile_set, row_ids, col_ids, starts, filled, panels)
    scale = 1.0 / math.sqrt(features.shape[1] * lax.axis_size("loop"))
    mix_one = to_nodes(forward_product(features, layout))
    z_one = jnp.einsum("de,dq->eq", weight_one, mix_one, preferred_element_type=jnp.float32)
    h_one = jax.nn.silu(z_one).astype(jnp.bfloat16)
    mix_two = to_nodes(forward_product(to_features(h_one), layout))
    z_two = jnp.einsum("de,dq->eq", weight_two, mix_two, preferred_element_type=jnp.float32)
    dz_two = (cotangent * silu_slope(z_two)).astype(jnp.bfloat16)
    grad_two = weight_grad(mix_two, dz_two) * scale
    dm_two = jnp.einsum("de,eq->dq", weight_two, dz_two, preferred_element_type=jnp.float32).astype(
        jnp.bfloat16
    )
    dh_one = to_nodes(transposed_product(to_features(dm_two), layout))
    dz_one = (dh_one * silu_slope(z_one)).astype(jnp.bfloat16)
    grad_one = weight_grad(mix_one, dz_one) * scale
    dm_one = jnp.einsum("de,eq->dq", weight_one, dz_one, preferred_element_type=jnp.float32).astype(
        jnp.bfloat16
    )
    partial_value = transposed_product(to_features(dm_one), layout)
    input_grad = lax.psum(partial_value.astype(jnp.bfloat16), "rep")
    return (grad_one, grad_two, input_grad)


def solution(mesh):
    return jax.shard_map(
        shards,
        mesh=mesh,
        in_specs=(
            P("feat", "loop"),
            P("loop", "rep", None, None, None),
            P("loop", "rep", None, None),
            P("loop", "rep", None),
            P(),
            P(),
            P(None, ("loop", "feat")),
        ),
        out_specs=(P(), P(), P("feat", "loop")),
        check_vma=False,
    )
```

profile of v0, /device:TPU:1, one launch (start us, length us, event | category | flops | bytes accessed | tf_op | source)
XLA Modules:
  0.0 1287.9 jit_solution(16373129460673330023)
XLA Ops:
  17.1 6.5 collective-permute-done.4
  30.8 51.0 %while.294 = (s32[]{:T(128)}, f32[32,8,128]{2,1,0:T(8,128)S(1)}, s32[]{:T(128)}, s32[]{:T(128)}, s32[112]{0:T(128)S(1)}, /*index=5*/s32[]{:T(128)}, bf16[112,128...) while((s32[]{:T(128)}, f32[32,8,128]{2,1,0:T(8,128)S(1)}, ...), condition=%wide.region_2.3_spmd.clone.clone, body=%wide.region_1.2_spmd.clone.clone.sunk | while | flops 11569371 | bytes 1516121 | solution.py:59
  81.9 95.8 %while.287 = (s32[]{:T(128)}, bf16[32,1024]{1,0:T(8,128)(2,1)S(1)}, f32[32,1024]{1,0:T(8,128)S(1)}, s32[8]{0:T(128)S(1)}, s32[8]{0:T(128)S(1)}, /*index=5*/s32[1...) while((s32[]{:T(128)}, bf16[32,1024]{1,0:T(8,128)(2,1)S(1)}, ...), condition=%wide.region_6.7_spmd, body=%wide.region_3.6_spmd.sunk | while | flops 11602160 | bytes 2565222 | solution.py:84
  89.7 6.4 while.298
  103.3 6.4 while.298
  116.9 6.4 while.298
  130.5 6.4 while.298
  144.1 6.4 while.298
  157.7 6.4 while.298
  171.3 6.4 while.298
  178.5 70.5 %all-reduce.7.cloned.1.call-done = bf16[32,4,256]{2,1,0:T(4,128)(2,1)} async-done(((bf16[32,4,256]{2,1,0:T(4,128)(2,1)}), bf16[32,4,256]{2,1,0:T(4,128)(2,1)}) %all-reduce.7.cloned.1.call-update) | async-done | bytes 65552 | tf_op jit(solution)/shard_map/psum | solution.py:109
  249.9 8.5 all_to_all.108
  258.6 6.5 all_to_all.109
  280.9 51.0 %while.295 = (s32[]{:T(128)}, f32[32,8,128]{2,1,0:T(8,128)S(1)}, s32[]{:T(128)}, s32[]{:T(128)}, s32[112]{0:T(128)S(1)}, /*index=5*/s32[]{:T(128)}, bf16[112,128...) while((s32[]{:T(128)}, f32[32,8,128]{2,1,0:T(8,128)S(1)}, ...), condition=%wide.region_9.10_spmd.clone.clone, body=%wide.region_8.9_spmd.clone.clone.sunk | while | flops 11569371 | bytes 1516121 | solution.py:59
  332.0 95.3 %while.289 = (s32[]{:T(128)}, bf16[32,1024]{1,0:T(8,128)(2,1)S(1)}, f32[32,1024]{1,0:T(8,128)S(1)}, s32[8]{0:T(128)S(1)}, s32[8]{0:T(128)S(1)}, /*index=5*/s32[1...) while((s32[]{:T(128)}, bf16[32,1024]{1,0:T(8,128)(2,1)S(1)}, ...), condition=%wide.region_13.14_spmd, body=%wide.region_10.13_spmd.sunk | while | flops 11602160 | bytes 2565222 | solution.py:84
  339.3 6.4 while.299
  352.9 6.4 while.299
  366.5 6.4 while.299
  380.1 6.4 while.299
  393.7 6.4 while.299
  407.3 6.4 while.299
  420.9 6.4 while.299
  428.1 73.9 %all-reduce.9.cloned.1.call-done = bf16[32,4,256]{2,1,0:T(4,128)(2,1)} async-done(((bf16[32,4,256]{2,1,0:T(4,128)(2,1)}), bf16[32,4,256]{2,1,0:T(4,128)(2,1)}) %all-reduce.9.cloned.1.call-update) | async-done | bytes 65552 | tf_op jit(solution)/shard_map/psum | solution.py:109
  502.8 8.5 all_to_all.110
  519.9 6.3 while.296
  526.2 128.6 %while.291 = (s32[]{:T(128)}, bf16[32,1024]{1,0:T(8,128)(2,1)S(1)}, s32[8]{0:T(128)S(1)}, s32[8]{0:T(128)S(1)}, bf16[32,1024]{1,0:T(8,128)(2,1)S(1)}, /*index=5*...) while((s32[]{:T(128)}, bf16[32,1024]{1,0:T(8,128)(2,1)S(1)}, ...), condition=%wide.region_20.21_spmd, body=%wide.region_17.20_spmd.sunk | while | flops 11667697 | bytes 2303082 | solution.py:100
  526.2 6.5 collective-permute-start.1
  534.7 6.3 while.300
  541.1 10.1 collective-permute-start.1
  563.4 6.3 while.300
  604.5 50.3 %while.300 = (s32[]{:T(128)}, f32[32,8,128]{2,1,0:T(8,128)S(1)}, s32[]{:T(128)}, s32[]{:T(128)}, s32[112]{0:T(128)S(1)}, /*index=5*/s32[]{:T(128)}, bf16[112,128...) while((s32[]{:T(128)}, f32[32,8,128]{2,1,0:T(8,128)S(1)}, ...), condition=%wide.region_19.19_spmd.clone.clone, body=%wide.region_18.18_spmd.clone.clone.sunk | while | flops 11569371 | bytes 1516121 | solution.py:59
  658.2 7.8 collective-permute-done.8
  672.1 60.1 %all-reduce.11.cloned.1.call-done = bf16[32,4,256]{2,0,1:T(8,128)(2,1)} async-done(((bf16[32,4,256]{2,0,1:T(8,128)(2,1)}), bf16[32,4,256]{2,0,1:T(8,128)(2,1)}) %all-reduce.11.cloned.1.call-update) | async-done | bytes 65552 | tf_op jit(solution)/shard_map/psum | solution.py:109
  732.2 9.2 all_to_all.111
  749.8 6.3 while.297
  756.1 129.7 %while.293 = (s32[]{:T(128)}, bf16[32,1024]{1,0:T(8,128)(2,1)S(1)}, s32[8]{0:T(128)S(1)}, s32[8]{0:T(128)S(1)}, bf16[32,1024]{1,0:T(8,128)(2,1)S(1)}, /*index=5*...) while((s32[]{:T(128)}, bf16[32,1024]{1,0:T(8,128)(2,1)S(1)}, ...), condition=%wide.region_29.30_spmd, body=%wide.region_26.29_spmd.sunk | while | flops 11667697 | bytes 2303082 | solution.py:100
  756.2 6.5 collective-permute-start
  764.6 6.4 while.301
  771.1 10.1 collective-permute-start
  783.1 6.4 while.301
  793.5 6.4 while.301
  803.8 6.4 while.301
  814.1 6.4 while.301
  824.5 6.4 while.301
  834.8 51.0 %while.301 = (s32[]{:T(128)}, f32[32,8,128]{2,1,0:T(8,128)S(1)}, s32[]{:T(128)}, s32[]{:T(128)}, s32[112]{0:T(128)S(1)}, /*index=5*/s32[]{:T(128)}, bf16[112,128...) while((s32[]{:T(128)}, f32[32,8,128]{2,1,0:T(8,128)S(1)}, ...), condition=%wide.region_28.28_spmd.clone.clone, body=%wide.region_27.27_spmd.clone.clone.sunk | while | flops 11569371 | bytes 1516121 | solution.py:59
  890.1 7.0 collective-permute-done.10
  903.2 327.0 %all-reduce.15.cloned.1.call-done = (f32[128,128]{1,0:T(8,128)}, f32[128,128]{1,0:T(8,128)}) async-done(((f32[128,128]{1,0:T(8,128)}, f32[128,128]{1,0:T(8,128)}), (f32[128,128]{1,0:T(8,128)}, f32[128,128]{1,0:T(8,128)})) %all-reduce.15.cloned.1.call-update) | async-done | bytes 131088 | tf_op jit(solution)/shard_map/psum | solution.py:119
  1231.7 48.2 %all-reduce.13.cloned.1.call-done = bf16[32,1024]{1,0:T(8,128)(2,1)} async-done(((bf16[32,1024]{1,0:T(8,128)(2,1)}), bf16[32,1024]{1,0:T(8,128)(2,1)}) %all-reduce.13.cloned.1.call-update) | async-done | bytes 65552 | tf_op jit(solution)/shard_map/psum | solution.py:148
  (953 shorter events, 605.6 us)
Async XLA Ops:
  7.2 251.2 %copy-start = (bf16[128,128]{1,0:T(8,128)(2,1)S(1)}, bf16[128,128]{1,0:T(8,128)(2,1)}, u32[]{:S(2)}) copy-start(bf16[128,128]{1,0:T(8,128)(2,1)} %param.35) | copy-start | bytes 98308
  7.2 241.8 %all-reduce.7.cloned.1.call-start = ((), (), s32[]{:S(2)}) async-start(), calls=%async_computation.6 | async-start | bytes 131072 | tf_op jit(solution)/shard_map/psum | solution.py:109
  7.2 16.4 %collective-permute-start.4 = (bf16[32,1024]{1,0:T(8,128)(2,1)}, bf16[32,1024]{1,0:T(8,128)(2,1)S(1)}, u32[]{:S(2)}, u32[]{:S(2)}) collective-permute-start(bf16[32,1024]{1,0:T(8,128)(2,1)} %param.31), channel_id=1, source_target_pairs={{0,16},{16,32},{32,48},{48,64},{64,80},{80,96},{96,112},{112,128},... | collective-permute-start | bytes 196616 | tf_op jit(solution)/shard_map/ppermute | solution.py:14
  24.5 6.2 collective-permute-start.5
  30.8 51.1 %copy-start.2 = (s32[1,1,8]{2,1,0:T(1,128)S(1)}, s32[1,1,8]{2,1,0:T(1,128)}, u32[]{:S(2)}) copy-start(s32[1,1,8]{2,1,0:T(1,128)} %param.34) | copy-start | bytes 100
  81.9 7.8 collective-permute-start.3
  96.2 7.1 collective-permute-start.3
  109.7 7.1 collective-permute-start.3
  123.3 7.1 collective-permute-start.3
  136.9 7.1 collective-permute-start.3
  150.5 7.1 collective-permute-start.3
  164.1 7.1 collective-permute-start.3
  178.4 323.5 %all-reduce.9.cloned.1.call-start = ((), (), s32[]{:S(2)}) async-start(), calls=%async_computation.7 | async-start | bytes 131072 | tf_op jit(solution)/shard_map/psum | solution.py:109
  265.1 9.6 collective-permute-start.6
  274.7 6.2 collective-permute-start.7
  332.0 179.3 %copy-start.1 = (bf16[128,128]{1,0:T(8,128)(2,1)S(1)}, bf16[128,128]{1,0:T(8,128)(2,1)}, u32[]{:S(2)}) copy-start(bf16[128,128]{1,0:T(8,128)(2,1)} %param.36) | copy-start | bytes 98308
  332.0 179.3 %copy-start.3 = (bf16[128,256]{1,0:T(8,128)(2,1)S(1)}, bf16[128,256]{1,0:T(8,128)(2,1)}, u32[]{:S(2)}) copy-start(bf16[128,256]{1,0:T(8,128)(2,1)} %param.37) | copy-start | bytes 196612
  332.1 7.3 collective-permute-start.2
  345.8 7.1 collective-permute-start.2
  359.4 7.1 collective-permute-start.2
  373.0 7.1 collective-permute-start.2
  386.6 7.1 collective-permute-start.2
  400.2 7.1 collective-permute-start.2
  413.8 7.1 collective-permute-start.2
  512.3 7.4 all-to-all-start.3
  516.5 215.8 %all-reduce.11.cloned.1.call-start = ((), (), s32[]{:S(2)}) async-start(), calls=%async_computation.8 | async-start | bytes 131072 | tf_op jit(solution)/shard_map/psum | solution.py:109
  526.2 14.8 %collective-permute-start.1 = (bf16[32,1024]{1,0:T(8,128)(2,1)S(1)}, bf16[32,1024]{1,0:T(8,128)(2,1)S(1)}, u32[]{:S(2)}, u32[]{:S(2)}) collective-permute-start(bf16[32,1024]{1,0:T(8,128)(2,1)S(1)} %get-tuple-element.3920), channel_id=1, source_target_pairs={{0,448},{16,464},{32,480},{48,496},{64,0},{80,16},{96,32},{112,48}... | collective-permute-start | bytes 196616 | tf_op jit(solution)/shard_map/while/body/eval_jaxpr/ppermute | solution.py:14
  541.1 18.4 %collective-permute-start.1 = (bf16[32,1024]{1,0:T(8,128)(2,1)S(1)}, bf16[32,1024]{1,0:T(8,128)(2,1)S(1)}, u32[]{:S(2)}, u32[]{:S(2)}) collective-permute-start(bf16[32,1024]{1,0:T(8,128)(2,1)S(1)} %get-tuple-element.3920), channel_id=1, source_target_pairs={{0,448},{16,464},{32,480},{48,496},{64,0},{80,16},{96,32},{112,48}... | collective-permute-start | bytes 196616 | tf_op jit(solution)/shard_map/while/body/eval_jaxpr/ppermute | solution.py:14
  559.5 10.2 collective-permute-start.1
  569.8 10.2 collective-permute-start.1
  580.1 10.2 collective-permute-start.1
  590.3 10.2 collective-permute-start.1
  600.6 54.2 %collective-permute-start.1 = (bf16[32,1024]{1,0:T(8,128)(2,1)S(1)}, bf16[32,1024]{1,0:T(8,128)(2,1)S(1)}, u32[]{:S(2)}, u32[]{:S(2)}) collective-permute-start(bf16[32,1024]{1,0:T(8,128)(2,1)S(1)} %get-tuple-element.3920), channel_id=1, source_target_pairs={{0,448},{16,464},{32,480},{48,496},{64,0},{80,16},{96,32},{112,48}... | collective-permute-start | bytes 196616 | tf_op jit(solution)/shard_map/while/body/eval_jaxpr/ppermute | solution.py:14
  654.9 11.1 collective-permute-start.8
  666.0 5.5 collective-permute-start.9
  742.3 7.4 all-to-all-start.5
  746.4 483.8 %all-reduce.15.cloned.1.call-start = ((), (), s32[]{:S(2)}) async-start(), calls=%async_computation.10 | async-start | bytes 262144 | tf_op jit(solution)/shard_map/psum | solution.py:119
  756.2 14.8 %collective-permute-start = (bf16[32,1024]{1,0:T(8,128)(2,1)S(1)}, bf16[32,1024]{1,0:T(8,128)(2,1)S(1)}, u32[]{:S(2)}, u32[]{:S(2)}) collective-permute-start(bf16[32,1024]{1,0:T(8,128)(2,1)S(1)} %get-tuple-element.4004), channel_id=1, source_target_pairs={{0,448},{16,464},{32,480},{48,496},{64,0},{80,16},{96,32},{112,48}... | collective-permute-start | bytes 196616 | tf_op jit(solution)/shard_map/while/body/eval_jaxpr/ppermute | solution.py:14
  771.1 18.5 %collective-permute-start = (bf16[32,1024]{1,0:T(8,128)(2,1)S(1)}, bf16[32,1024]{1,0:T(8,128)(2,1)S(1)}, u32[]{:S(2)}, u32[]{:S(2)}) collective-permute-start(bf16[32,1024]{1,0:T(8,128)(2,1)S(1)} %get-tuple-element.4004), channel_id=1, source_target_pairs={{0,448},{16,464},{32,480},{48,496},{64,0},{80,16},{96,32},{112,48}... | collective-permute-start | bytes 196616 | tf_op jit(solution)/shard_map/while/body/eval_jaxpr/ppermute | solution.py:14
  789.6 10.3 collective-permute-start
  799.9 10.3 collective-permute-start
  810.3 10.3 collective-permute-start
  820.6 10.3 collective-permute-start
  830.9 54.9 %collective-permute-start = (bf16[32,1024]{1,0:T(8,128)(2,1)S(1)}, bf16[32,1024]{1,0:T(8,128)(2,1)S(1)}, u32[]{:S(2)}, u32[]{:S(2)}) collective-permute-start(bf16[32,1024]{1,0:T(8,128)(2,1)S(1)} %get-tuple-element.4004), channel_id=1, source_target_pairs={{0,448},{16,464},{32,480},{48,496},{64,0},{80,16},{96,32},{112,48}... | collective-permute-start | bytes 196616 | tf_op jit(solution)/shard_map/while/body/eval_jaxpr/ppermute | solution.py:14
  885.8 11.3 collective-permute-start.10
  897.1 5.4 collective-permute-start.11
  900.5 379.4 %all-reduce.13.cloned.1.call-start = ((), (), s32[]{:S(2)}) async-start(), calls=%async_computation.9 | async-start | bytes 131072 | tf_op jit(solution)/shard_map/psum | solution.py:148
Sparse Core Ops, SparseCore 0:
  178.6 70.4 all-reduce.6
  428.2 73.7 all-reduce.8
  672.3 59.9 all-reduce.10
  900.7 329.5 all-reduce.14
  1232.4 47.5 all-reduce.12
where the time goes:
time: 1280 us; the launch traced here: 1290 us
  waiting for transfers between devices  663 us (52%)
  local copies, waits for them, and re-layouts  314 us (25%)
  starting transfers between devices  122 us (10%)
  other arithmetic  84 us (7%)
  blocking collectives  32.6 us (3%)
  matrix products  32.4 us (3%)
  loops' own time  25.1 us (2%)
  between operations  15.5 us (1%)
    psum x1, waiting for transfers between devices, weight_grad(): return lax.psum(part_sum, ('loop', 'feat'))  327 us
    psum x3, waiting for transfers between devices, to_nodes(): summed = lax.psum(partial_value.astype(jnp.bfloat16), 'rep')  205 us
    gather x60, local copies, waits for them, and re-layouts, one_round(): chosen = tile_set[slot_ids]  158 us
    ppermute x36, starting transfers between devices, passed_along(): return lax.ppermute(value, axis, pairs)  114 us
    ppermute x36, waiting for transfers between devices, passed_along(): return lax.ppermute(value, axis, pairs)  77.1 us
    psum x1, waiting for transfers between devices, shards(): input_grad = lax.psum(partial_value.astype(jnp.bfloat16), 'rep')  48.2 us
    lt x60, other arithmetic, one_round(): alive_mask = within < number  40 us
    gather x60, local copies, waits for them, and re-layouts, one_round(): picked = shaped[:, row_ids[slot_ids], :]  36.2 us
  transfers between devices with their start and end apart: 43, of which 29 were waited for; matrix products, arithmetic and copies ran while one was open for 17% of the time, Pallas kernels for 0%

commit v1 on v0

v1 whole, which is shorter than its diff:
```python
import functools
import math

import jax
import jax.numpy as jnp
from jax import lax
from jax.experimental import pallas as pl
from jax.experimental.pallas import tpu as pltpu
from jax.sharding import PartitionSpec as P

MESH = pl.DeviceIdType.MESH
BF16 = jnp.bfloat16
F32 = jnp.float32


def place_kernel(row_ids, col_ids, starts, ends, tiles, out):
    section = pl.program_id(0)
    side = tiles.shape[-1]
    per_chunk = out.shape[-1] // side
    out[...] = jnp.zeros_like(out)

    def one_tile(slot, carry):
        row = pl.multiple_of(row_ids[slot] * side, side)
        col = col_ids[slot]
        lane = pl.multiple_of(lax.rem(col, per_chunk) * side, side)
        out[0, lax.div(col, per_chunk), pl.ds(row, side), pl.ds(lane, side)] = tiles[slot]
        return carry

    lax.fori_loop(starts[section], ends[section], one_tile, 0)


def dense_sections(tile_set, row_ids, col_ids, starts, ends, chunks, nodes):
    sections = starts.shape[0]
    width = nodes // chunks
    return pl.pallas_call(
        place_kernel,
        out_shape=jax.ShapeDtypeStruct((sections, chunks, nodes, width), BF16),
        grid_spec=pltpu.PrefetchScalarGridSpec(
            num_scalar_prefetch=4,
            grid=(sections,),
            in_specs=[pl.BlockSpec(tile_set.shape, lambda k, *_: (0, 0, 0))],
            out_specs=pl.BlockSpec((1, chunks, nodes, width), lambda k, *_: (k, 0, 0, 0)),
        ),
        name="place_tiles",
    )(row_ids, col_ids, starts, ends, tile_set)


def nt_dot(a, b):
    return lax.dot_general(a, b, (((1,), (1,)), ((), ())), preferred_element_type=F32)


def nn_dot(a, b):
    return lax.dot_general(a, b, (((1,), (0,)), ((), ())), preferred_element_type=F32)


def slope_of(z):
    s = 1.0 / (1.0 + jnp.exp(-z))
    return s * (1.0 + z * (1.0 - s))


def layers_kernel(
    sizes,
    feat_ref, dense_hbm, w1, w1t, w2, w2t, cot_ref,
    out_ref, g1_ref, g2_ref,
    dense, hbuf, acc, pst, ebuf, fin, lst, dmb, dmf, z1, mix, rd, ru, sd, su,
    asem, ringr, fs, bs, xs, xr, ls, dmr, p0s, rdr, rur, ds, us,
):
    L, R, F = sizes
    S = L // R
    H = S // 2
    half = F // 2
    C = hbuf.shape[-1]
    i, r, f = lax.axis_index("loop"), lax.axis_index("rep"), lax.axis_index("feat")

    def at_loop(value):
        return lax.rem(value + L, L)

    up, dn = at_loop(i + R), at_loop(i - R)
    ahead, behind = at_loop(i + r), at_loop(i - r)

    def local(src, dst, sem):
        return pltpu.make_async_copy(src, dst, sem)

    def remote(src, dst, ssem, rsem, to):
        return pltpu.make_async_remote_copy(
            src_ref=src, dst_ref=dst, send_sem=ssem, recv_sem=rsem,
            device_id=to, device_id_type=MESH,
        )

    def done(ref, sem):
        pltpu.make_async_copy(ref, ref, sem).wait()

    order = [0]
    for s in range(1, H):
        order += [s, S - s]
    order += [H]
    for k in order:
        local(dense_hbm.at[k], dense.at[k], asem.at[k]).start()

    barrier = pltpu.get_barrier_semaphore()

    def greet(*to):
        pl.semaphore_signal(barrier, inc=1, device_id=to, device_id_type=MESH)

    greet(up, r, f)
    greet(dn, r, f)
    for a in range(R):
        for b in range(F):
            if (a, b) != (0, 0):
                greet(i, lax.rem(r + a, R), lax.rem(f + b, F))

    @pl.when(r != 0)
    def _():
        for b in range(F):
            greet(behind, r, b)

    for a in range(1, R):
        for b in range(F):
            greet(at_loop(i + a), a, b)
    zero = jnp.zeros(rd.shape[3:], BF16)
    for p in range(2):
        for q in range(F):
            if q >= half:
                rd[p, 0, q] = zero
            else:
                ru[p, 0, q] = zero
    pl.semaphore_wait(barrier, 1 + R * F + jnp.where(r != 0, F + R * F, 0))

    for q in range(F):
        src = feat_ref.at[:, pl.ds(q * C, C)]

        @pl.when(r == 0)
        def _():
            local(src, hbuf.at[0, 0, q], ringr.at[0, 0, q]).start()

        @pl.when(r != 0)
        def _():
            remote(src, hbuf.at[0, 0, q], p0s.at[q], ringr.at[0, 0, q], (ahead, r, f)).start()

    def forward(p):
        def send_up(k, q):
            return remote(hbuf.at[p, k, q], hbuf.at[p, k + 1, q], fs.at[p, k, q], ringr.at[p, k + 1, q], (up, r, f))

        def send_dn(k, s, q):
            to = S - 1 - s
            return remote(hbuf.at[p, k, q], hbuf.at[p, to, q], bs.at[p, s, q], ringr.at[p, to, q], (dn, r, f))

        def term(k, q):
            return nt_dot(hbuf[p, k, q], dense[k, q])

        if p == 0:
            done(dense.at[0], asem.at[0])

        def first(q, carry):
            done(hbuf.at[p, 0, q], ringr.at[p, 0, q])
            send_up(0, q).start()
            send_dn(0, 0, q).start()

            @pl.when(q == 0)
            def _():
                acc[...] = term(0, q)

            @pl.when(q != 0)
            def _():
                acc[...] += term(0, q)

            return carry

        lax.fori_loop(0, F, first, 0)

        def stage(s, carry):
            kb = S - s
            if p == 0:
                done(dense.at[s], asem.at[s])
                done(dense.at[kb], asem.at[kb])

            def chunk(q, inner):
                done(hbuf.at[p, s, q], ringr.at[p, s, q])

                @pl.when((s < H - 1) | (q < half))
                def _():
                    send_up(s, q).start()

                done(hbuf.at[p, kb, q], ringr.at[p, kb, q])

                @pl.when((s < H - 1) | (q >= half))
                def _():
                    send_dn(kb, s, q).start()

                acc[...] += term(s, q) + term(kb, q)
                return inner

            return lax.fori_loop(0, F, chunk, carry)

        lax.fori_loop(1, H, stage, 0)
        if p == 0:
            done(dense.at[H], asem.at[H])

        def last(q, carry):
            done(hbuf.at[p, H, q], ringr.at[p, H, q])
            acc[...] += term(H, q)
            return carry

        lax.fori_loop(0, F, last, 0)
        for q in range(F):
            pst[p, q] = acc[:, q * C:(q + 1) * C].astype(BF16)
        for a in range(R):
            for b in range(F):
                rr, q = lax.rem(r + a, R), lax.rem(f + b, F)
                if (a, b) == (0, 0):
                    local(pst.at[p, q], ebuf.at[p, r, f], xr.at[p, r, f]).start()
                else:
                    remote(pst.at[p, q], ebuf.at[p, r, f], xs.at[p, a, b], xr.at[p, r, f], (i, rr, q)).start()

    def gathered(e):
        total = None
        for a in range(R):
            for b in range(F):
                done(ebuf.at[e, a, b], xr.at[e, a, b])
        for a in range(R):
            part = ebuf[e, a].reshape(z1.shape).astype(F32)
            total = part if total is None else total + part
        return total.astype(BF16)

    def spread(n, value, to_loop, dst, sem, shifted):
        lst[n] = value.reshape(lst.shape[1:])
        for b in range(F):
            ff = lax.rem(f + b, F)

            def away():
                remote(lst.at[n, ff], dst.at[f], ls.at[n, ff], sem.at[f], (to_loop, r, ff)).start()

            def here():
                local(lst.at[n, ff], dst.at[f], sem.at[f]).start()

            if b:
                away()
            elif shifted:
                pl.when(r == 0)(here)
                pl.when(r != 0)(away)
            else:
                here()

    def transposed(p):
        for q in range(F):
            done(dmb.at[p, q], dmr.at[p, q])
            dmf[:, q * C:(q + 1) * C] = dmb[p, q]

        def send_dn(s, q):
            return remote(sd.at[p, s, q], rd.at[p, s, q], ds.at[p, s, q], rdr.at[p, s, q], (dn, r, f))

        def send_up(s, q):
            return remote(su.at[p, s, q], ru.at[p, s, q], us.at[p, s, q], rur.at[p, s, q], (up, r, f))

        def first(q, carry):
            value = nn_dot(dmf[...], dense[H, q]).astype(BF16)

            @pl.when(q < half)
            def _():
                sd[p, 0, q] = value
                send_dn(0, q).start()

            @pl.when(q >= half)
            def _():
                su[p, 0, q] = value
                send_up(0, q).start()

            return carry

        lax.fori_loop(0, F, first, 0)

        def stage(s, carry):
            def chunk(q, inner):
                down = nn_dot(dmf[...], dense[H - s, q])
                above = nn_dot(dmf[...], dense[H + s, q])

                @pl.when((s > 1) | (q < half))
                def _():
                    done(rd.at[p, s - 1, q], rdr.at[p, s - 1, q])

                sd[p, s, q] = (down + rd[p, s - 1, q].astype(F32)).astype(BF16)
                send_dn(s, q).start()

                @pl.when((s > 1) | (q >= half))
                def _():
                    done(ru.at[p, s - 1, q], rur.at[p, s - 1, q])

                su[p, s, q] = (above + ru[p, s - 1, q].astype(F32)).astype(BF16)
                send_up(s, q).start()
                return inner

            return lax.fori_loop(0, F, chunk, carry)

        lax.fori_loop(1, H, stage, 0)
        x = 2 + p

        def last(q, carry):
            own = nn_dot(dmf[...], dense[0, q])
            done(rd.at[p, H - 1, q], rdr.at[p, H - 1, q])
            done(ru.at[p, H - 1, q], rur.at[p, H - 1, q])
            own = own + rd[p, H - 1, q].astype(F32) + ru[p, H - 1, q].astype(F32)
            pst[x, q] = own.astype(BF16)
            for a in range(R):
                rr = lax.rem(r + a, R)
                if p == 0:
                    dst, sem, to, mine = ebuf.at[2, r, f], xr.at[2, r, f], (behind, rr, q), (r == 0) & (q == f)
                else:
                    dst, sem, to, mine = fin.at[r, q], xr.at[3, r, q], (behind, rr, f), r == 0

                def away():
                    remote(pst.at[x, q], dst, xs.at[x, a, q], sem, to).start()

                if a:
                    away()
                else:
                    pl.when(mine)(lambda: local(pst.at[x, q], dst, sem).start())
                    pl.when(jnp.logical_not(mine))(away)
            return carry

        lax.fori_loop(0, F, last, 0)

    forward(0)
    mix_one = gathered(0)
    mix[0] = mix_one
    z_one = nn_dot(w1t[...], mix_one)
    z1[...] = z_one
    h_one = (z_one / (1.0 + jnp.exp(-z_one))).astype(BF16)
    spread(0, h_one, ahead, hbuf.at[1, 0], ringr.at[1, 0], True)
    forward(1)
    mix_two = gathered(1)
    mix[1] = mix_two
    z_two = nn_dot(w2t[...], mix_two)
    dz_two = (cot_ref[...].astype(F32) * slope_of(z_two)).astype(BF16)
    spread(1, nn_dot(w2[...], dz_two).astype(BF16), i, dmb.at[0], dmr.at[0], False)
    g2_ref[...] = nt_dot(mix[1], dz_two)
    transposed(0)
    dh_one = gathered(2)
    dz_one = (dh_one.astype(F32) * slope_of(z1[...])).astype(BF16)
    spread(2, nn_dot(w1[...], dz_one).astype(BF16), i, dmb.at[1], dmr.at[1], False)
    g1_ref[...] = nt_dot(mix[0], dz_one)
    transposed(1)
    for a in range(R):
        for q in range(F):
            done(fin.at[a, q], xr.at[3, a, q])
    for q in range(F):
        total = fin[0, q].astype(F32)
        for a in range(1, R):
            total = total + fin[a, q].astype(F32)
        out_ref[:, q * C:(q + 1) * C] = total.astype(BF16)

    one = pst.at[0, 0]

    @pl.when(r != 0)
    def _():
        for q in range(F):
            done(one, p0s.at[q])

    for p in range(2):
        def sent_chunk(n, carry):
            s, q = lax.div(n, F), lax.rem(n, F)

            @pl.when((s < H - 1) | (q < half))
            def _():
                done(one, fs.at[p, s, q])

            @pl.when((s < H - 1) | (q >= half))
            def _():
                done(one, bs.at[p, s, q])

            @pl.when((s > 0) | (q < half))
            def _():
                done(one, ds.at[p, s, q])

            @pl.when((s > 0) | (q >= half))
            def _():
                done(one, us.at[p, s, q])

            return carry

        lax.fori_loop(0, H * F, sent_chunk, 0)
    for a in range(R):
        for b in range(F):
            if (a, b) != (0, 0):
                done(one, xs.at[0, a, b])
                done(one, xs.at[1, a, b])
            if a:
                done(one, xs.at[2, a, b])
                done(one, xs.at[3, a, b])

    for b in range(F):
        pl.when(jnp.logical_not((r == 0) & (f == b)))(functools.partial(done, one, xs.at[2, 0, b]))
        pl.when(r != 0)(functools.partial(done, one, xs.at[3, 0, b]))
        pl.when(jnp.logical_not((r == 0) & (f == b)))(functools.partial(done, one, ls.at[0, b]))
        pl.when(f != b)(functools.partial(done, one, ls.at[1, b]))
        pl.when(f != b)(functools.partial(done, one, ls.at[2, b]))


def shards(features, tile_values, tile_coords, section_counts, weight_one, weight_two, cotangent):
    L, R, F = (lax.axis_size(n) for n in ("loop", "rep", "feat"))
    S = L // R
    H = S // 2
    tile_set = tile_values[0, 0]
    d, nodes = features.shape
    D = weight_one.shape[0]
    C = nodes // F
    filled = section_counts[0, 0]
    slots = tile_set.shape[0]
    ends = jnp.cumsum(filled)
    starts = jnp.minimum(ends - filled, slots)
    ends = jnp.minimum(ends, slots)
    dense = dense_sections(tile_set, tile_coords[0, 0, 0], tile_coords[0, 0, 1], starts, ends, F, nodes)
    scale = 1.0 / math.sqrt(nodes * L)
    vmem = pl.BlockSpec(memory_space=pltpu.VMEM)
    dma = pltpu.SemaphoreType.DMA
    input_grad, g1, g2 = pl.pallas_call(
        functools.partial(layers_kernel, (L, R, F)),
        out_shape=(
            jax.ShapeDtypeStruct((d, nodes), BF16),
            jax.ShapeDtypeStruct((D, D), F32),
            jax.ShapeDtypeStruct((D, D), F32),
        ),
        in_specs=[vmem, pl.BlockSpec(memory_space=pl.ANY)] + [vmem] * 5,
        out_specs=(vmem,) * 3,
        scratch_shapes=[
            pltpu.VMEM((S, F, nodes, C), BF16),
            pltpu.VMEM((2, S, F, d, C), BF16),
            pltpu.VMEM((d, nodes), F32),
            pltpu.VMEM((4, F, d, C), BF16),
            pltpu.VMEM((3, R, F, d, C), BF16),
            pltpu.VMEM((R, F, d, C), BF16),
            pltpu.VMEM((3, F, d, C), BF16),
            pltpu.VMEM((2, F, d, C), BF16),
            pltpu.VMEM((d, nodes), BF16),
            pltpu.VMEM((D, C), F32),
            pltpu.VMEM((2, D, C), BF16),
        ]
        + [pltpu.VMEM((2, H, F, d, C), BF16)] * 4
        + [
            dma((S,)), dma((2, S, F)), dma((2, H, F)), dma((2, H, F)),
            dma((4, R, F)), dma((4, R, F)), dma((3, F)), dma((2, F)), dma((F,)),
            dma((2, H, F)), dma((2, H, F)), dma((2, H, F)), dma((2, H, F)),
        ],
        compiler_params=pltpu.CompilerParams(
            collective_id=0, has_side_effects=True, vmem_limit_bytes=48 * 1024 * 1024
        ),
        name="layers",
    )(features, dense, weight_one, weight_one.T, weight_two, weight_two.T, cotangent)
    g1, g2 = lax.psum((g1 * scale, g2 * scale), ("loop", "feat"))
    return (g1, g2, input_grad)


def solution(mesh):
    return jax.shard_map(
        shards,
        mesh=mesh,
        in_specs=(
            P("feat", "loop"),
            P("loop", "rep", None, None, None),
            P("loop", "rep", None, None),
            P("loop", "rep", None),
            P(),
            P(),
            P(None, ("loop", "feat")),
        ),
        out_specs=(P(), P(), P("feat", "loop")),
        check_vma=False,
    )
```

time: 1280 us -> 488 us (0.38)
  waiting for transfers between devices: 663 us -> 322 us
  local copies, waits for them, and re-layouts: 314 us -> 6.6 us
  Pallas kernels: 0 us -> 141 us
  starting transfers between devices: 122 us -> 0.04 us
  other arithmetic: 84 us -> 2.77 us
  blocking collectives: 32.6 us -> 0 us
  matrix products: 32.4 us -> 0 us
  loops' own time: 25.1 us -> 0 us
    gather x240 -> x0, local copies, waits for them, and re-layouts: 270 us -> none  [the longest x60 158 us: one_round(): chosen = tile_set[slot_ids]]
    psum x5 -> x1, waiting for transfers between devices: 580 us -> 322 us  [shards(): g1, g2 = lax.psum((g1 * scale, g2 * scale), ('loop', 'feat'))]
    pallas_call x0 -> x2, Pallas kernels: none -> 141 us  [the longest x1 131 us: shards(): pl.pallas_call(functools.partial(layers_kernel, (L, R, F)), out_shape=(ja...]
    ppermute x36 -> x0, starting transfers between devices: 114 us -> none  [passed_along(): return lax.ppermute(value, axis, pairs)]
    ppermute x36 -> x0, waiting for transfers between devices: 77.1 us -> none  [passed_along(): return lax.ppermute(value, axis, pairs)]
    lt x60 -> x0, other arithmetic: 40 us -> none  [one_round(): alive_mask = within < number]
    select_n x124 -> x0, other arithmetic: 38.3 us -> none  [the longest x30 18.8 us: one_round(): target = col_ids[slot_ids]]
    dynamic_slice x56 -> x0, local copies, waits for them, and re-layouts: 34.6 us -> none  [the longest x28 17.8 us: section_term(): number = jnp.where(enabled, filled[section_id], 0)]
  transfers between devices with their start and end apart: 43 -> 1, of which waited for: 29 -> 1; matrix products, arithmetic and copies ran while one was open for 17% -> 0% of each run, Pallas kernels for 0% -> 0%
where the time goes in v1:
time: 488 us; the launch traced here: 486 us
  waiting for transfers between devices  322 us (66%)
  Pallas kernels  141 us (29%)
  between operations  14.1 us (3%)
  local copies, waits for them, and re-layouts  6.6 us (1%)
    psum x1, waiting for transfers between devices, shards(): g1, g2 = lax.psum((g1 * scale, g2 * scale), ('loop', 'feat'))  322 us
    pallas_call x1, Pallas kernels, shards(): pl.pallas_call(functools.partial(layers_kernel, (L, R, F)), out_shape=(ja...  131 us
    pallas_call x1, Pallas kernels, dense_sections(): pl.pallas_call(place_kernel, out_shape=jax.ShapeDtypeStruct((sections, ch...  10.2 us
  transfers between devices with their start and end apart: 1, of which 1 were waited for; matrix products, arithmetic and copies ran while one was open for 0% of the time, Pallas kernels for 0%

profile of v1, /device:TPU:1, one launch (start us, length us, event | category | flops | bytes accessed | tf_op | source)
XLA Modules:
  0.0 486.4 jit_solution(1221980671107202863)
XLA Ops:
  7.2 0.0 copy-start
  7.2 0.0 copy-start.1
  7.2 0.0 copy-start.3
  7.2 0.0 copy-start.2
  7.2 0.0 all-reduce.3.cloned.1.call-start
  7.3 0.9 reduce-window.9
  8.1 1.2 bitcast_minimum_fusion
  9.4 1.3 slice_bitcast_fusion
  10.6 0.9 copy.10
  11.5 0.9 copy.11
  12.4 10.2 %place_tiles.1.dense_hbm = bf16[8,4,1024,256]{3,2,1,0:T(8,128)(2,1)} custom-call(s32[112]{0:T(128)} %get-tuple-element.12.row_ids, s32[112]{0:T(128)} %get-tuple-element.11.col_ids, s32[8]{0:T(128)} %get-tuple-element.14.starts, s32[8]{0:T(128)} %get-tuple-element.13.ends, bf16[112,128,128]{2,1,0:T(8,128)(2,1)} %bitcast.17), custom_call_target="tpu_custom_call" | custom-call | tf_op jit(solution)/shard_map/place_tiles/pallas_call | solution.py:35
  22.6 0.0 copy-done
  22.6 0.0 copy-done.1
  22.6 0.0 copy-done.3
  22.6 0.0 copy-done.2
  22.6 130.9 %layers.1 = (bf16[32,1024]{1,0:T(8,128)(2,1)S(1)}, f32[128,128]{1,0:T(8,128)S(1)}, f32[128,128]{1,0:T(8,128)S(1)}) custom-call(bf16[32,1024]{1,0:T(8,128)(2,1)S(1)} %copy-done.2, bf16[8,4,1024,256]{3,2,1,0:T(8,128)(2,1)} %place_tiles.1.dense_hbm, bf16[128,128]{1,0:T(8,128)(2,1)S(1)} %copy-done, bf16[128,128]{1,0:T(8,128)(2,1)S(1)} %bitcast.15, ...), custom_call_target="tpu_custom_call" | custom-call | tf_op jit(solution)/shard_map/layers/pallas_call | solution.py:415
  153.5 0.7 broadcast_multiply_fusion
  154.2 0.0 all-reduce.3.cloned.1.call-update
  154.2 321.7 %all-reduce.3.cloned.1.call-done = (f32[128,128]{1,0:T(8,128)}, f32[128,128]{1,0:T(8,128)}) async-done(((f32[128,128]{1,0:T(8,128)}, f32[128,128]{1,0:T(8,128)}), (f32[128,128]{1,0:T(8,128)}, f32[128,128]{1,0:T(8,128)})) %all-reduce.3.cloned.1.call-update) | async-done | bytes 131088 | tf_op jit(solution)/shard_map/psum | solution.py:448
  475.9 1.5 copy.15
  477.4 1.5 copy.16
  478.9 0.6 copy.17
Async XLA Ops:
  7.2 15.4 %copy-start = (bf16[128,128]{1,0:T(8,128)(2,1)S(1)}, bf16[128,128]{1,0:T(8,128)(2,1)}, u32[]{:S(2)}) copy-start(bf16[128,128]{1,0:T(8,128)(2,1)} %w1.1) | copy-start | bytes 98308
  7.2 15.4 %copy-start.1 = (bf16[128,128]{1,0:T(8,128)(2,1)S(1)}, bf16[128,128]{1,0:T(8,128)(2,1)}, u32[]{:S(2)}) copy-start(bf16[128,128]{1,0:T(8,128)(2,1)} %w2.1) | copy-start | bytes 98308
  7.2 15.4 %copy-start.3 = (bf16[128,256]{1,0:T(8,128)(2,1)S(1)}, bf16[128,256]{1,0:T(8,128)(2,1)}, u32[]{:S(2)}) copy-start(bf16[128,256]{1,0:T(8,128)(2,1)} %cot_ref.1) | copy-start | bytes 196612
  7.2 15.4 %copy-start.2 = (bf16[32,1024]{1,0:T(8,128)(2,1)S(1)}, bf16[32,1024]{1,0:T(8,128)(2,1)}, u32[]{:S(2)}) copy-start(bf16[32,1024]{1,0:T(8,128)(2,1)} %feat_ref.1) | copy-start | bytes 196612
  7.2 468.7 %all-reduce.3.cloned.1.call-start = ((), (), s32[]{:S(2)}) async-start(), calls=%async_computation | async-start | bytes 262144 | tf_op jit(solution)/shard_map/psum | solution.py:448
Sparse Core Ops, SparseCore 0:
  154.3 321.5 all-reduce.2

commit v2 on v1

--- a/solution.py
+++ b/solution.py
@@ -13,36 +13,48 @@
 F32 = jnp.float32
 
 
-def place_kernel(row_ids, col_ids, starts, ends, tiles, out):
-    section = pl.program_id(0)
-    side = tiles.shape[-1]
+def place_kernel(coords, counts, tiles_hbm, out, tiles, sem):
+    copy = pltpu.make_async_copy(tiles_hbm.at[0, 0], tiles, sem)
+    copy.start()
+    slots, side = tiles.shape[:2]
+    sections = out.shape[0]
     per_chunk = out.shape[-1] // side
-    out[...] = jnp.zeros_like(out)
-
-    def one_tile(slot, carry):
-        row = pl.multiple_of(row_ids[slot] * side, side)
-        col = col_ids[slot]
-        lane = pl.multiple_of(lax.rem(col, per_chunk) * side, side)
-        out[0, lax.div(col, per_chunk), pl.ds(row, side), pl.ds(lane, side)] = tiles[slot]
+
+    def clear(n, carry):
+        out[n] = jnp.zeros(out.shape[1:], out.dtype)
         return carry
 
-    lax.fori_loop(starts[section], ends[section], one_tile, 0)
-
-
-def dense_sections(tile_set, row_ids, col_ids, starts, ends, chunks, nodes):
-    sections = starts.shape[0]
-    width = nodes // chunks
+    lax.fori_loop(0, sections, clear, 0)
+    copy.wait()
+
+    def one_section(section, start):
+        end = jnp.minimum(start + counts[0, 0, section], slots)
+
+        def one_tile(slot, carry):
+            row = pl.multiple_of(coords[0, 0, 0, slot] * side, side)
+            col = coords[0, 0, 1, slot]
+            lane = pl.multiple_of(lax.rem(col, per_chunk) * side, side)
+            out[section, lax.div(col, per_chunk), pl.ds(row, side), pl.ds(lane, side)] = tiles[slot]
+            return carry
+
+        lax.fori_loop(start, end, one_tile, 0)
+        return end
+
+    lax.fori_loop(0, sections, one_section, 0)
+
+
+def dense_sections(tile_values, tile_coords, section_counts, chunks, nodes):
+    sections = section_counts.shape[-1]
+    smem = pl.BlockSpec(memory_space=pltpu.SMEM)
     return pl.pallas_call(
         place_kernel,
-        out_shape=jax.ShapeDtypeStruct((sections, chunks, nodes, width), BF16),
-        grid_spec=pltpu.PrefetchScalarGridSpec(
-            num_scalar_prefetch=4,
-            grid=(sections,),
-            in_specs=[pl.BlockSpec(tile_set.shape, lambda k, *_: (0, 0, 0))],
-            out_specs=pl.BlockSpec((1, chunks, nodes, width), lambda k, *_: (k, 0, 0, 0)),
-        ),
+        out_shape=jax.ShapeDtypeStruct((sections, chunks, nodes, nodes // chunks), BF16),
+        in_specs=[smem, smem, pl.BlockSpec(memory_space=pltpu.HBM)],
+        out_specs=pl.BlockSpec(memory_space=pltpu.VMEM),
+        scratch_shapes=[pltpu.VMEM(tile_values.shape[2:], BF16), pltpu.SemaphoreType.DMA],
+        compiler_params=pltpu.CompilerParams(vmem_limit_bytes=8 * 1024 * 1024),
         name="place_tiles",
-    )(row_ids, col_ids, starts, ends, tile_set)
+    )(tile_coords, section_counts, tile_values)
 
 
 def nt_dot(a, b):
@@ -59,11 +71,11 @@
 
 
 def layers_kernel(
-    sizes,
-    feat_ref, dense_hbm, w1, w1t, w2, w2t, cot_ref,
+    sizes, scale,
+    feat_ref, dense, w1, w2, cot_ref,
     out_ref, g1_ref, g2_ref,
-    dense, hbuf, acc, pst, ebuf, fin, lst, dmb, dmf, z1, mix, rd, ru, sd, su,
-    asem, ringr, fs, bs, xs, xr, ls, dmr, p0s, rdr, rur, ds, us,
+    hbuf, acc, pst, ebuf, fin, lst, dmb, dmf, z1, mix, rd, ru, sd, su, wt, gst, gin, gring, gsum, gall,
+    gss, gsr, gus, gds, grr, gas, gar, ringr, fs, bs, xs, xr, ls, dmr, p0s, rdr, rur, ds, us,
 ):
     L, R, F = sizes
     S = L // R
@@ -77,6 +89,8 @@
 
     up, dn = at_loop(i + R), at_loop(i - R)
     ahead, behind = at_loop(i + r), at_loop(i - r)
+    block, me = lax.div(i, R), lax.rem(i, R)
+    first_of_block = block * R
 
     def local(src, dst, sem):
         return pltpu.make_async_copy(src, dst, sem)
@@ -89,13 +103,6 @@
 
     def done(ref, sem):
         pltpu.make_async_copy(ref, ref, sem).wait()
-
-    order = [0]
-    for s in range(1, H):
-        order += [s, S - s]
-    order += [H]
-    for k in order:
-        local(dense_hbm.at[k], dense.at[k], asem.at[k]).start()
 
     barrier = pltpu.get_barrier_semaphore()
 
@@ -117,6 +124,9 @@
     for a in range(1, R):
         for b in range(F):
             greet(at_loop(i + a), a, b)
+    for a in range(1, R):
+        for b in range(F):
+            greet(first_of_block + lax.rem(me + a, R), r, b)
     zero = jnp.zeros(rd.shape[3:], BF16)
     for p in range(2):
         for q in range(F):
@@ -124,7 +134,9 @@
                 rd[p, 0, q] = zero
             else:
                 ru[p, 0, q] = zero
-    pl.semaphore_wait(barrier, 1 + R * F + jnp.where(r != 0, F + R * F, 0))
+    wt[0] = w1[...].T
+    wt[1] = w2[...].T
+    pl.semaphore_wait(barrier, 1 + R * F + (R - 1) * F + jnp.where(r != 0, F + R * F, 0))
 
     for q in range(F):
         src = feat_ref.at[:, pl.ds(q * C, C)]
@@ -147,9 +159,6 @@
 
         def term(k, q):
             return nt_dot(hbuf[p, k, q], dense[k, q])
-
-        if p == 0:
-            done(dense.at[0], asem.at[0])
 
         def first(q, carry):
             done(hbuf.at[p, 0, q], ringr.at[p, 0, q])
@@ -170,10 +179,6 @@
 
         def stage(s, carry):
             kb = S - s
-            if p == 0:
-                done(dense.at[s], asem.at[s])
-                done(dense.at[kb], asem.at[kb])
-
             def chunk(q, inner):
                 done(hbuf.at[p, s, q], ringr.at[p, s, q])
 
@@ -193,9 +198,6 @@
             return lax.fori_loop(0, F, chunk, carry)
 
         lax.fori_loop(1, H, stage, 0)
-        if p == 0:
-            done(dense.at[H], asem.at[H])
-
         def last(q, carry):
             done(hbuf.at[p, H, q], ringr.at[p, H, q])
             acc[...] += term(H, q)
@@ -241,6 +243,68 @@
             else:
                 here()
 
+    def grad_start(g, value):
+        gst[g] = value.reshape(gst.shape[1:])
+        for a in range(R):
+            for b in range(F):
+                c, ff = lax.rem(me + a, R), lax.rem(f + b, F)
+                if (a, b) == (0, 0):
+                    local(gst.at[g, r, f], gin.at[g, me, f], gsr.at[g, me, f]).start()
+                else:
+                    to = (first_of_block + c, r, ff)
+                    remote(gst.at[g, r, ff], gin.at[g, me, f], gss.at[g, a, b], gsr.at[g, me, f], to).start()
+
+    def grad_up(g, s):
+        slot = lax.rem(block + S - s, S)
+        return remote(gring.at[g, slot], gring.at[g, slot], gus.at[g, s], grr.at[g, slot], (up, r, f))
+
+    def grad_dn(g, s):
+        slot = lax.rem(block + s, S)
+        return remote(gring.at[g, slot], gring.at[g, slot], gds.at[g, s], grr.at[g, slot], (dn, r, f))
+
+    def grad_block(g):
+        total = None
+        for a in range(R):
+            for b in range(F):
+                done(gin.at[g, a, b], gsr.at[g, a, b])
+        for a in range(R):
+            for b in range(F):
+                total = gin[g, a, b] if total is None else total + gin[g, a, b]
+        gring[g, block] = total
+        grad_up(g, 0).start()
+        grad_dn(g, 0).start()
+
+    def grad_hop(g, s):
+        below, above = lax.rem(block + S - s, S), lax.rem(block + s, S)
+        done(gring.at[g, below], grr.at[g, below])
+        grad_up(g, s).start()
+        done(gring.at[g, above], grr.at[g, above])
+
+        @pl.when(s < H - 1)
+        def _():
+            grad_dn(g, s).start()
+
+    def grad_spread(g):
+        far = lax.rem(block + H, S)
+        done(gring.at[g, far], grr.at[g, far])
+        total = gring[g, 0]
+        for n in range(1, S):
+            total = total + gring[g, n]
+        gsum[g] = total * scale
+        for a in range(R):
+            for b in range(F):
+                if (a, b) == (0, 0):
+                    local(gsum.at[g], gall.at[g, r, f], gar.at[g, r, f]).start()
+                else:
+                    to = (i, lax.rem(r + a, R), lax.rem(f + b, F))
+                    remote(gsum.at[g], gall.at[g, r, f], gas.at[g, a, b], gar.at[g, r, f], to).start()
+
+    def grad_end(g, ref):
+        for a in range(R):
+            for b in range(F):
+                done(gall.at[g, a, b], gar.at[g, a, b])
+        ref[...] = gall[g].reshape(ref.shape)
+
     def transposed(p):
         for q in range(F):
             done(dmb.at[p, q], dmr.at[p, q])
@@ -268,6 +332,7 @@
             return carry
 
         lax.fori_loop(0, F, first, 0)
+        grad_block(p)
 
         def stage(s, carry):
             def chunk(q, inner):
@@ -289,7 +354,9 @@
                 send_up(s, q).start()
                 return inner
 
-            return lax.fori_loop(0, F, chunk, carry)
+            lax.fori_loop(0, F, chunk, carry)
+            grad_hop(p, s)
+            return carry
 
         lax.fori_loop(1, H, stage, 0)
         x = 2 + p
@@ -318,26 +385,27 @@
             return carry
 
         lax.fori_loop(0, F, last, 0)
+        grad_spread(p)
 
     forward(0)
     mix_one = gathered(0)
     mix[0] = mix_one
-    z_one = nn_dot(w1t[...], mix_one)
+    z_one = nn_dot(wt[0], mix_one)
     z1[...] = z_one
     h_one = (z_one / (1.0 + jnp.exp(-z_one))).astype(BF16)
     spread(0, h_one, ahead, hbuf.at[1, 0], ringr.at[1, 0], True)
     forward(1)
     mix_two = gathered(1)
     mix[1] = mix_two
-    z_two = nn_dot(w2t[...], mix_two)
+    z_two = nn_dot(wt[1], mix_two)
     dz_two = (cot_ref[...].astype(F32) * slope_of(z_two)).astype(BF16)
     spread(1, nn_dot(w2[...], dz_two).astype(BF16), i, dmb.at[0], dmr.at[0], False)
-    g2_ref[...] = nt_dot(mix[1], dz_two)
+    grad_start(0, nt_dot(mix[1], dz_two))
     transposed(0)
     dh_one = gathered(2)
     dz_one = (dh_one.astype(F32) * slope_of(z1[...])).astype(BF16)
     spread(2, nn_dot(w1[...], dz_one).astype(BF16), i, dmb.at[1], dmr.at[1], False)
-    g1_ref[...] = nt_dot(mix[0], dz_one)
+    grad_start(1, nt_dot(mix[0], dz_one))
     transposed(1)
     for a in range(R):
         for q in range(F):
@@ -348,6 +416,9 @@
             total = total + fin[a, q].astype(F32)
         out_ref[:, q * C:(q + 1) * C] = total.astype(BF16)
 
+    grad_end(0, g2_ref)
+    grad_end(1, g1_ref)
+
     one = pst.at[0, 0]
 
     @pl.when(r != 0)
@@ -378,6 +449,16 @@
             return carry
 
         lax.fori_loop(0, H * F, sent_chunk, 0)
+        piece = gsum.at[0]
+        for s in range(H):
+            done(piece, gus.at[p, s])
+            if s < H - 1:
+                done(piece, gds.at[p, s])
+        for a in range(R):
+            for b in range(F):
+                if (a, b) != (0, 0):
+                    done(piece, gss.at[p, a, b])
+                    done(piece, gas.at[p, a, b])
     for a in range(R):
         for b in range(F):
             if (a, b) != (0, 0):
@@ -399,30 +480,24 @@
     L, R, F = (lax.axis_size(n) for n in ("loop", "rep", "feat"))
     S = L // R
     H = S // 2
-    tile_set = tile_values[0, 0]
     d, nodes = features.shape
     D = weight_one.shape[0]
     C = nodes // F
-    filled = section_counts[0, 0]
-    slots = tile_set.shape[0]
-    ends = jnp.cumsum(filled)
-    starts = jnp.minimum(ends - filled, slots)
-    ends = jnp.minimum(ends, slots)
-    dense = dense_sections(tile_set, tile_coords[0, 0, 0], tile_coords[0, 0, 1], starts, ends, F, nodes)
+    piece = D // (R * F)
+    dense = dense_sections(tile_values, tile_coords, section_counts, F, nodes)
     scale = 1.0 / math.sqrt(nodes * L)
     vmem = pl.BlockSpec(memory_space=pltpu.VMEM)
     dma = pltpu.SemaphoreType.DMA
     input_grad, g1, g2 = pl.pallas_call(
-        functools.partial(layers_kernel, (L, R, F)),
+        functools.partial(layers_kernel, (L, R, F), scale),
         out_shape=(
             jax.ShapeDtypeStruct((d, nodes), BF16),
             jax.ShapeDtypeStruct((D, D), F32),
             jax.ShapeDtypeStruct((D, D), F32),
         ),
-        in_specs=[vmem, pl.BlockSpec(memory_space=pl.ANY)] + [vmem] * 5,
+        in_specs=[vmem] * 5,
         out_specs=(vmem,) * 3,
         scratch_shapes=[
-            pltpu.VMEM((S, F, nodes, C), BF16),
             pltpu.VMEM((2, S, F, d, C), BF16),
             pltpu.VMEM((d, nodes), F32),
             pltpu.VMEM((4, F, d, C), BF16),
@@ -436,16 +511,22 @@
         ]
         + [pltpu.VMEM((2, H, F, d, C), BF16)] * 4
         + [
-            dma((S,)), dma((2, S, F)), dma((2, H, F)), dma((2, H, F)),
+            pltpu.VMEM((2, D, D), BF16),
+            pltpu.VMEM((2, R, F, piece, D), F32),
+            pltpu.VMEM((2, R, F, piece, D), F32),
+            pltpu.VMEM((2, S, piece, D), F32),
+            pltpu.VMEM((2, piece, D), F32),
+            pltpu.VMEM((2, R, F, piece, D), F32),
+            dma((2, R, F)), dma((2, R, F)), dma((2, H)), dma((2, H)), dma((2, S)), dma((2, R, F)), dma((2, R, F)),
+            dma((2, S, F)), dma((2, H, F)), dma((2, H, F)),
             dma((4, R, F)), dma((4, R, F)), dma((3, F)), dma((2, F)), dma((F,)),
             dma((2, H, F)), dma((2, H, F)), dma((2, H, F)), dma((2, H, F)),
         ],
         compiler_params=pltpu.CompilerParams(
-            collective_id=0, has_side_effects=True, vmem_limit_bytes=48 * 1024 * 1024
+            collective_id=0, has_side_effects=True, vmem_limit_bytes=24 * 1024 * 1024
         ),
         name="layers",
-    )(features, dense, weight_one, weight_one.T, weight_two, weight_two.T, cotangent)
-    g1, g2 = lax.psum((g1 * scale, g2 * scale), ("loop", "feat"))
+    )(features, dense, weight_one, weight_two, cotangent)
     return (g1, g2, input_grad)
 
 

time: 488 us -> 147 us (0.30)
  the two profiles are of different devices: /device:TPU:1 before, /device:TPU:16 now
where the time goes in v2:
time: 147 us
  Pallas kernels  141 us (96%)
  local copies, waits for them, and re-layouts  5.27 us (4%)
    pallas_call x1, Pallas kernels, shards(): pl.pallas_call(functools.partial(layers_kernel, (L, R, F), scale), out_sh...  137 us
    unnamed x17, local copies, waits for them, and re-layouts  5.27 us
    pallas_call x1, Pallas kernels, dense_sections(): pl.pallas_call(place_kernel, out_shape=jax.ShapeDtypeStruct((sections, ch...  3.35 us

profile of v2, /device:TPU:16, one launch (start us, length us, event | category | flops | bytes accessed | tf_op | source)
XLA Modules:
  0.0 146.5 jit_solution(12909564125357651390)
XLA Ops:
  0.6 0.0 copy-start
  0.6 2.0 %copy-done = bf16[1,1,112,128,128]{4,3,2,1,0:T(8,128)(2,1)S(1)} copy-done((bf16[1,1,112,128,128]{4,3,2,1,0:T(8,128)(2,1)S(1)}, bf16[1,1,112,128,128]{4,3,2,1,0:T(8,128)(2,1)}, u32[]{:S(2)}) %copy-start) | copy-done | bytes 3670040
  2.7 0.0 copy-start.5
  2.7 0.7 copy-done.5
  3.4 0.0 copy-start.6
  3.4 0.7 copy-done.6
  4.0 0.0 copy-start.1
  4.0 0.0 copy-start.2
  4.0 0.0 copy-start.3
  4.0 0.0 copy-start.4
  4.0 3.4 %place_tiles.1.dense = bf16[8,4,1024,256]{3,2,1,0:T(8,128)(2,1)S(1)} custom-call(s32[1,1,2,112]{3,2,1,0:T(2,128)S(1)} %copy-done.5, s32[1,1,8]{2,1,0:T(1,128)S(1)} %copy-done.6, bf16[1,1,112,128,128]{4,3,2,1,0:T(8,128)(2,1)S(1)} %copy-done), custom_call_target="tpu_custom_call" | custom-call | tf_op jit(solution)/shard_map/place_tiles/pallas_call | solution.py:49
  7.4 0.0 copy-done.1
  7.4 0.0 copy-done.2
  7.4 0.0 copy-done.3
  7.4 0.0 copy-done.4
  7.4 137.2 %layers.1 = (bf16[32,1024]{1,0:T(8,128)(2,1)S(1)}, f32[128,128]{1,0:T(8,128)S(1)}, f32[128,128]{1,0:T(8,128)S(1)}) custom-call(bf16[32,1024]{1,0:T(8,128)(2,1)S(1)} %copy-done.1, bf16[8,4,1024,256]{3,2,1,0:T(8,128)(2,1)S(1)} %place_tiles.1.dense, bf16[128,128]{1,0:T(8,128)(2,1)S(1)} %copy-done.3, bf16[128,128]{1,0:T(8,128)(2,1)S(1)} %copy-done.4, ...), custom_call_target="tpu_custom_call" | custom-call | tf_op jit(solution)/shard_map/layers/pallas_call | solution.py:491
  144.6 0.6 copy.13
  145.2 0.6 copy.14
  145.9 0.6 copy.15
Async XLA Ops:
  0.6 2.0 %copy-start = (bf16[1,1,112,128,128]{4,3,2,1,0:T(8,128)(2,1)S(1)}, bf16[1,1,112,128,128]{4,3,2,1,0:T(8,128)(2,1)}, u32[]{:S(2)}) copy-start(bf16[1,1,112,128,128]{4,3,2,1,0:T(8,128)(2,1)} %tiles_hbm.1) | copy-start | bytes 11010052
  2.7 0.7 copy-start.5
  3.4 0.7 copy-start.6
  4.0 3.4 %copy-start.1 = (bf16[32,1024]{1,0:T(8,128)(2,1)S(1)}, bf16[32,1024]{1,0:T(8,128)(2,1)}, u32[]{:S(2)}) copy-start(bf16[32,1024]{1,0:T(8,128)(2,1)} %feat_ref.1) | copy-start | bytes 196612
  4.0 3.4 %copy-start.2 = (bf16[128,256]{1,0:T(8,128)(2,1)S(1)}, bf16[128,256]{1,0:T(8,128)(2,1)}, u32[]{:S(2)}) copy-start(bf16[128,256]{1,0:T(8,128)(2,1)} %cot_ref.1) | copy-start | bytes 196612
  4.0 3.4 %copy-start.3 = (bf16[128,128]{1,0:T(8,128)(2,1)S(1)}, bf16[128,128]{1,0:T(8,128)(2,1)}, u32[]{:S(2)}) copy-start(bf16[128,128]{1,0:T(8,128)(2,1)} %w1.1) | copy-start | bytes 98308
  4.0 3.4 %copy-start.4 = (bf16[128,128]{1,0:T(8,128)(2,1)S(1)}, bf16[128,128]{1,0:T(8,128)(2,1)}, u32[]{:S(2)}) copy-start(bf16[128,128]{1,0:T(8,128)(2,1)} %w2.1) | copy-start | bytes 98308

commit v3 on v2

v3 whole, which is shorter than its diff:
```python
import functools
import math

import jax
import jax.numpy as jnp
from jax import lax
from jax.experimental import pallas as pl
from jax.experimental.pallas import tpu as pltpu
from jax.sharding import PartitionSpec as P

MESH = pl.DeviceIdType.MESH
BF16 = jnp.bfloat16
F32 = jnp.float32


def place_kernel(coords_hbm, counts_hbm, tiles_hbm, out, coords, counts, tiles, sems):
    pairs = ((coords_hbm, coords), (counts_hbm, counts), (tiles_hbm.at[0, 0], tiles))
    copies = [pltpu.make_async_copy(src, dst, sems.at[n]) for n, (src, dst) in enumerate(pairs)]
    for copy in copies:
        copy.start()
    slots, side = tiles.shape[:2]
    sections = out.shape[0]
    per_chunk = out.shape[-1] // side

    def clear(n, carry):
        out[n] = jnp.zeros(out.shape[1:], out.dtype)
        return carry

    lax.fori_loop(0, sections, clear, 0)
    for copy in copies:
        copy.wait()

    def one_section(section, start):
        end = jnp.minimum(start + counts[0, 0, section], slots)

        def one_tile(slot, carry):
            row = pl.multiple_of(coords[0, 0, 0, slot] * side, side)
            col = coords[0, 0, 1, slot]
            lane = pl.multiple_of(lax.rem(col, per_chunk) * side, side)
            out[section, lax.div(col, per_chunk), pl.ds(row, side), pl.ds(lane, side)] = tiles[slot]
            return carry

        lax.fori_loop(start, end, one_tile, 0)
        return end

    lax.fori_loop(0, sections, one_section, 0)


def dense_sections(tile_values, tile_coords, section_counts, chunks, nodes):
    sections = section_counts.shape[-1]
    hbm = pl.BlockSpec(memory_space=pltpu.HBM)
    return pl.pallas_call(
        place_kernel,
        out_shape=jax.ShapeDtypeStruct((sections, chunks, nodes, nodes // chunks), BF16),
        in_specs=[hbm] * 3,
        out_specs=pl.BlockSpec(memory_space=pltpu.VMEM),
        scratch_shapes=[
            pltpu.SMEM(tile_coords.shape, jnp.int32),
            pltpu.SMEM(section_counts.shape, jnp.int32),
            pltpu.VMEM(tile_values.shape[2:], BF16),
            pltpu.SemaphoreType.DMA((3,)),
        ],
        compiler_params=pltpu.CompilerParams(vmem_limit_bytes=8 * 1024 * 1024),
        name="place_tiles",
    )(*(pltpu.with_memory_space_constraint(a, pltpu.HBM) for a in (tile_coords, section_counts, tile_values)))


def nt_dot(a, b):
    return lax.dot_general(a, b, (((1,), (1,)), ((), ())), preferred_element_type=F32)


def nn_dot(a, b):
    return lax.dot_general(a, b, (((1,), (0,)), ((), ())), preferred_element_type=F32)


def slope_of(z):
    s = 1.0 / (1.0 + jnp.exp(-z))
    return s * (1.0 + z * (1.0 - s))


def layers_kernel(
    sizes, scale,
    feat_ref, dense, w1, w2, cot_ref,
    out_ref, g1_ref, g2_ref,
    hbuf, acc, pst, ebuf, fin, lst, dmb, dmf, z1, mix, rd, ru, sd, su, wt, gst, gin, gring, gsum, gall,
    gss, gsr, gus, grr, gas, gar, ringr, fs, bs, xs, xr, ls, dmr, p0s, h0s, rdr, rur, ds, us,
):
    L, R, F = sizes
    S = L // R
    H = S // 2
    half = F // 2
    far_first = sorted(range(R), key=lambda a: -min(a, R - a))
    C = hbuf.shape[-1]
    i, r, f = lax.axis_index("loop"), lax.axis_index("rep"), lax.axis_index("feat")

    def at_loop(value):
        return lax.rem(value + 2 * L, L)

    up, dn = at_loop(i + R), at_loop(i - R)
    up2, dn2 = at_loop(i + 2 * R), at_loop(i - 2 * R)
    ahead, behind = at_loop(i + r), at_loop(i - r)
    block, me = lax.div(i, R), lax.rem(i, R)
    first_of_block = block * R

    def local(src, dst, sem):
        return pltpu.make_async_copy(src, dst, sem)

    def remote(src, dst, ssem, rsem, to):
        return pltpu.make_async_remote_copy(
            src_ref=src, dst_ref=dst, send_sem=ssem, recv_sem=rsem,
            device_id=to, device_id_type=MESH,
        )

    def done(ref, sem):
        pltpu.make_async_copy(ref, ref, sem).wait()

    barrier = pltpu.get_barrier_semaphore()

    def greet(*to):
        pl.semaphore_signal(barrier, inc=1, device_id=to, device_id_type=MESH)

    for m in range(1, S):
        greet(at_loop(i + m * R), r, f)
    for b in range(F):
        greet(at_loop(behind - R), r, b)
        greet(at_loop(behind + R), r, b)
    for a in range(R):
        for b in range(F):
            if (a, b) != (0, 0):
                greet(i, lax.rem(r + a, R), lax.rem(f + b, F))

    @pl.when(r != 0)
    def _():
        for b in range(F):
            greet(behind, r, b)

    for a in range(1, R):
        for b in range(F):
            greet(at_loop(i + a), a, b)
    for a in range(1, R):
        for b in range(F):
            greet(first_of_block + lax.rem(me + a, R), r, b)
    zero = jnp.zeros(rd.shape[3:], BF16)
    for p in range(2):
        for q in range(F):
            if q >= half:
                rd[p, 1, q] = zero
            else:
                ru[p, 1, q] = zero
    wt[0] = w1[...].T
    wt[1] = w2[...].T
    pl.semaphore_wait(barrier, S - 1 + 2 * F + R * F - 1 + (R - 1) * F + jnp.where(r != 0, F + R * F, 0))

    def to_ring(p, src, q, ssem, ff):
        for n, (k, to) in enumerate(((1, at_loop(ahead + R)), (S - 1, at_loop(ahead - R)), (0, ahead))):
            def away(n=n, k=k, to=to):
                remote(src, hbuf.at[p, k, q], ssem.at[n], ringr.at[p, k, q], (to, r, ff)).start()

            def here(k=k):
                local(src, hbuf.at[p, k, q], ringr.at[p, k, q]).start()

            if k:
                away()
            else:
                mine = (r == 0) & (ff == f)
                pl.when(mine)(here)
                pl.when(jnp.logical_not(mine))(away)

    for q in range(F):
        to_ring(0, feat_ref.at[:, pl.ds(q * C, C)], q, p0s.at[q], f)

    def forward(p):
        def hop(k, to_k, q, ssem, to):
            remote(hbuf.at[p, k, q], hbuf.at[p, to_k, q], ssem, ringr.at[p, to_k, q], (to, r, f)).start()

        def here(k, q):
            done(hbuf.at[p, k, q], ringr.at[p, k, q])

        def term(k, q):
            return nt_dot(hbuf[p, k, q], dense[k, q])

        def near(q, carry):
            here(1, q)
            hop(1, 2, q, fs.at[p, 0, q], up)
            here(S - 1, q)
            hop(S - 1, S - 2, q, bs.at[p, 0, q], dn)
            here(0, q)
            value = term(0, q) + term(1, q) + term(S - 1, q)

            @pl.when(q == 0)
            def _():
                acc[...] = value

            @pl.when(q != 0)
            def _():
                acc[...] += value

            return carry

        lax.fori_loop(0, F, near, 0)

        def middle(q, carry):
            here(2, q)

            @pl.when(q < half)
            def _():
                hop(2, H, q, fs.at[p, 2, q], up2)

            hop(2, 3, q, fs.at[p, 1, q], up)
            here(S - 2, q)

            @pl.when(q >= half)
            def _():
                hop(S - 2, H, q, bs.at[p, 2, q], dn2)

            hop(S - 2, S - 3, q, bs.at[p, 1, q], dn)
            acc[...] += term(2, q) + term(S - 2, q)
            return carry

        lax.fori_loop(0, F, middle, 0)

        def far(q, carry):
            here(3, q)
            here(S - 3, q)
            here(H, q)
            acc[...] += term(3, q) + term(S - 3, q) + term(H, q)
            return carry

        lax.fori_loop(0, F, far, 0)
        for q in range(F):
            pst[p, q] = acc[:, q * C:(q + 1) * C].astype(BF16)
        for a in far_first:
            for b in range(F):
                rr, q = lax.rem(r + a, R), lax.rem(f + b, F)
                if (a, b) == (0, 0):
                    local(pst.at[p, q], ebuf.at[p, r, f], xr.at[p, r, f]).start()
                else:
                    remote(pst.at[p, q], ebuf.at[p, r, f], xs.at[p, a, b], xr.at[p, r, f], (i, rr, q)).start()

    def gathered(e):
        total = None
        for a in range(R):
            for b in range(F):
                done(ebuf.at[e, a, b], xr.at[e, a, b])
        for a in range(R):
            part = ebuf[e, a].reshape(z1.shape).astype(F32)
            total = part if total is None else total + part
        return total.astype(BF16)

    def spread(n, value, dst, sem):
        lst[n] = value.reshape(lst.shape[1:])
        for b in range(F):
            ff = lax.rem(f + b, F)
            if n == 0:
                to_ring(1, lst.at[n, ff], f, h0s.at[ff], ff)
            elif b:
                remote(lst.at[n, ff], dst.at[f], ls.at[n, ff], sem.at[f], (i, r, ff)).start()
            else:
                local(lst.at[n, ff], dst.at[f], sem.at[f]).start()

    def grad_start(g, value):
        gst[g] = value.reshape(gst.shape[1:])
        for a in range(R):
            for b in range(F):
                c, ff = lax.rem(me + a, R), lax.rem(f + b, F)
                if (a, b) == (0, 0):
                    local(gst.at[g, r, f], gin.at[g, me, f], gsr.at[g, me, f]).start()
                else:
                    to = (first_of_block + c, r, ff)
                    remote(gst.at[g, r, ff], gin.at[g, me, f], gss.at[g, a, b], gsr.at[g, me, f], to).start()

    def grad_send(g, m):
        slot = gring.at[g, block]
        return remote(slot, slot, gus.at[g, m], grr.at[g, block], (at_loop(i + m * R), r, f))

    def grad_block(g):
        total = None
        for a in range(R):
            for b in range(F):
                done(gin.at[g, a, b], gsr.at[g, a, b])
        for a in range(R):
            for b in range(F):
                total = gin[g, a, b] if total is None else total + gin[g, a, b]
        gring[g, block] = total
        for m in range(1, S):
            grad_send(g, m).start()

    def grad_spread(g):
        for m in range(1, S):
            other = lax.rem(block + m, S)
            done(gring.at[g, other], grr.at[g, other])
        total = gring[g, 0]
        for n in range(1, S):
            total = total + gring[g, n]
        gsum[g] = total * scale
        for a in range(R):
            for b in range(F):
                if (a, b) == (0, 0):
                    local(gsum.at[g], gall.at[g, r, f], gar.at[g, r, f]).start()
                else:
                    to = (i, lax.rem(r + a, R), lax.rem(f + b, F))
                    remote(gsum.at[g], gall.at[g, r, f], gas.at[g, a, b], gar.at[g, r, f], to).start()

    def grad_end(g, ref):
        for a in range(R):
            for b in range(F):
                done(gall.at[g, a, b], gar.at[g, a, b])
        ref[...] = gall[g].reshape(ref.shape)

    def transposed(p):
        for q in range(F):
            done(dmb.at[p, q], dmr.at[p, q])
            dmf[:, q * C:(q + 1) * C] = dmb[p, q]

        def send_dn(s, q, to=dn):
            remote(sd.at[p, s, q], rd.at[p, s, q], ds.at[p, s, q], rdr.at[p, s, q], (to, r, f)).start()

        def send_up(s, q, to=up):
            remote(su.at[p, s, q], ru.at[p, s, q], us.at[p, s, q], rur.at[p, s, q], (to, r, f)).start()

        def term(k, q):
            return nn_dot(dmf[...], dense[k, q])

        def from_dn(s, q):
            done(rd.at[p, s, q], rdr.at[p, s, q])

        def from_up(s, q):
            done(ru.at[p, s, q], rur.at[p, s, q])

        def far(q, carry):
            value = term(H, q).astype(BF16)

            @pl.when(q < half)
            def _():
                sd[p, 1, q] = value
                send_dn(1, q, dn2)

            @pl.when(q >= half)
            def _():
                su[p, 1, q] = value
                send_up(1, q, up2)

            sd[p, 0, q] = term(3, q).astype(BF16)
            send_dn(0, q)
            su[p, 0, q] = term(S - 3, q).astype(BF16)
            send_up(0, q)
            return carry

        lax.fori_loop(0, F, far, 0)

        def middle(q, carry):
            down, above = term(2, q), term(S - 2, q)
            from_dn(0, q)
            pl.when(q < half)(lambda: from_dn(1, q))
            sd[p, 2, q] = (down + rd[p, 0, q].astype(F32) + rd[p, 1, q].astype(F32)).astype(BF16)
            send_dn(2, q)
            from_up(0, q)
            pl.when(q >= half)(lambda: from_up(1, q))
            su[p, 2, q] = (above + ru[p, 0, q].astype(F32) + ru[p, 1, q].astype(F32)).astype(BF16)
            send_up(2, q)
            return carry

        lax.fori_loop(0, F, middle, 0)
        grad_block(p)

        def near(q, carry):
            down, above = term(1, q), term(S - 1, q)
            from_dn(2, q)
            sd[p, 3, q] = (down + rd[p, 2, q].astype(F32)).astype(BF16)
            send_dn(3, q)
            from_up(2, q)
            su[p, 3, q] = (above + ru[p, 2, q].astype(F32)).astype(BF16)
            send_up(3, q)
            return carry

        lax.fori_loop(0, F, near, 0)
        x = 2 + p

        def last(q, carry):
            own = nn_dot(dmf[...], dense[0, q])
            done(rd.at[p, H - 1, q], rdr.at[p, H - 1, q])
            done(ru.at[p, H - 1, q], rur.at[p, H - 1, q])
            own = own + rd[p, H - 1, q].astype(F32) + ru[p, H - 1, q].astype(F32)
            pst[x, q] = own.astype(BF16)
            for a in far_first:
                rr = lax.rem(r + a, R)
                if p == 0:
                    dst, sem, to, mine = ebuf.at[2, r, f], xr.at[2, r, f], (behind, rr, q), (r == 0) & (q == f)
                else:
                    dst, sem, to, mine = fin.at[r, q], xr.at[3, r, q], (behind, rr, f), r == 0

                def away():
                    remote(pst.at[x, q], dst, xs.at[x, a, q], sem, to).start()

                if a:
                    away()
                else:
                    pl.when(mine)(lambda: local(pst.at[x, q], dst, sem).start())
                    pl.when(jnp.logical_not(mine))(away)
            return carry

        lax.fori_loop(0, F, last, 0)
        grad_spread(p)

    forward(0)
    mix_one = gathered(0)
    mix[0] = mix_one
    z_one = nn_dot(wt[0], mix_one)
    z1[...] = z_one
    h_one = (z_one / (1.0 + jnp.exp(-z_one))).astype(BF16)
    spread(0, h_one, None, None)
    forward(1)
    mix_two = gathered(1)
    mix[1] = mix_two
    z_two = nn_dot(wt[1], mix_two)
    dz_two = (cot_ref[...].astype(F32) * slope_of(z_two)).astype(BF16)
    spread(1, nn_dot(w2[...], dz_two).astype(BF16), dmb.at[0], dmr.at[0])
    grad_start(0, nt_dot(mix[1], dz_two))
    transposed(0)
    dh_one = gathered(2)
    dz_one = (dh_one.astype(F32) * slope_of(z1[...])).astype(BF16)
    spread(2, nn_dot(w1[...], dz_one).astype(BF16), dmb.at[1], dmr.at[1])
    grad_start(1, nt_dot(mix[0], dz_one))
    transposed(1)
    for a in range(R):
        for q in range(F):
            done(fin.at[a, q], xr.at[3, a, q])
    for q in range(F):
        total = fin[0, q].astype(F32)
        for a in range(1, R):
            total = total + fin[a, q].astype(F32)
        out_ref[:, q * C:(q + 1) * C] = total.astype(BF16)

    grad_end(0, g2_ref)
    grad_end(1, g1_ref)

    one = pst.at[0, 0]

    for q in range(F):
        for n in range(2):
            done(one, p0s.at[q, n])
            done(one, h0s.at[q, n])
        pl.when(r != 0)(functools.partial(done, one, p0s.at[q, 2]))
        pl.when(jnp.logical_not((r == 0) & (f == q)))(functools.partial(done, one, h0s.at[q, 2]))

    for p in range(2):
        def sent_chunk(n, carry):
            s, q = lax.div(n, F), lax.rem(n, F)

            @pl.when((s < 2) | (q < half))
            def _():
                done(one, fs.at[p, s, q])

            @pl.when((s < 2) | (q >= half))
            def _():
                done(one, bs.at[p, s, q])

            return carry

        lax.fori_loop(0, 3 * F, sent_chunk, 0)

        def sent_sum(n, carry):
            s, q = lax.div(n, F), lax.rem(n, F)

            @pl.when((s != 1) | (q < half))
            def _():
                done(one, ds.at[p, s, q])

            @pl.when((s != 1) | (q >= half))
            def _():
                done(one, us.at[p, s, q])

            return carry

        lax.fori_loop(0, 4 * F, sent_sum, 0)
        piece = gsum.at[0]
        for m in range(1, S):
            done(piece, gus.at[p, m])
        for a in range(R):
            for b in range(F):
                if (a, b) != (0, 0):
                    done(piece, gss.at[p, a, b])
                    done(piece, gas.at[p, a, b])
    for a in range(R):
        for b in range(F):
            if (a, b) != (0, 0):
                done(one, xs.at[0, a, b])
                done(one, xs.at[1, a, b])
            if a:
                done(one, xs.at[2, a, b])
                done(one, xs.at[3, a, b])

    for b in range(F):
        pl.when(jnp.logical_not((r == 0) & (f == b)))(functools.partial(done, one, xs.at[2, 0, b]))
        pl.when(r != 0)(functools.partial(done, one, xs.at[3, 0, b]))
        pl.when(f != b)(functools.partial(done, one, ls.at[1, b]))
        pl.when(f != b)(functools.partial(done, one, ls.at[2, b]))


def shards(features, tile_values, tile_coords, section_counts, weight_one, weight_two, cotangent):
    L, R, F = (lax.axis_size(n) for n in ("loop", "rep", "feat"))
    S = L // R
    H = S // 2
    d, nodes = features.shape
    D = weight_one.shape[0]
    C = nodes // F
    piece = D // (R * F)
    dense = dense_sections(tile_values, tile_coords, section_counts, F, nodes)
    scale = 1.0 / math.sqrt(nodes * L)
    vmem = pl.BlockSpec(memory_space=pltpu.VMEM)
    dma = pltpu.SemaphoreType.DMA
    input_grad, g1, g2 = pl.pallas_call(
        functools.partial(layers_kernel, (L, R, F), scale),
        out_shape=(
            jax.ShapeDtypeStruct((d, nodes), BF16),
            jax.ShapeDtypeStruct((D, D), F32),
            jax.ShapeDtypeStruct((D, D), F32),
        ),
        in_specs=[vmem] * 5,
        out_specs=(vmem,) * 3,
        scratch_shapes=[
            pltpu.VMEM((2, S, F, d, C), BF16),
            pltpu.VMEM((d, nodes), F32),
            pltpu.VMEM((4, F, d, C), BF16),
            pltpu.VMEM((3, R, F, d, C), BF16),
            pltpu.VMEM((R, F, d, C), BF16),
            pltpu.VMEM((3, F, d, C), BF16),
            pltpu.VMEM((2, F, d, C), BF16),
            pltpu.VMEM((d, nodes), BF16),
            pltpu.VMEM((D, C), F32),
            pltpu.VMEM((2, D, C), BF16),
        ]
        + [pltpu.VMEM((2, H, F, d, C), BF16)] * 4
        + [
            pltpu.VMEM((2, D, D), BF16),
            pltpu.VMEM((2, R, F, piece, D), F32),
            pltpu.VMEM((2, R, F, piece, D), F32),
            pltpu.VMEM((2, S, piece, D), F32),
            pltpu.VMEM((2, piece, D), F32),
            pltpu.VMEM((2, R, F, piece, D), F32),
            dma((2, R, F)), dma((2, R, F)), dma((2, S)), dma((2, S)), dma((2, R, F)), dma((2, R, F)),
            dma((2, S, F)), dma((2, 3, F)), dma((2, 3, F)),
            dma((4, R, F)), dma((4, R, F)), dma((3, F)), dma((2, F)), dma((F, 3)), dma((F, 3)),
            dma((2, H, F)), dma((2, H, F)), dma((2, H, F)), dma((2, H, F)),
        ],
        compiler_params=pltpu.CompilerParams(
            collective_id=0, has_side_effects=True, vmem_limit_bytes=24 * 1024 * 1024
        ),
        name="layers",
    )(features, dense, weight_one, weight_two, cotangent)
    return (g1, g2, input_grad)


def solution(mesh):
    return jax.shard_map(
        shards,
        mesh=mesh,
        in_specs=(
            P("feat", "loop"),
            P("loop", "rep", None, None, None),
            P("loop", "rep", None, None),
            P("loop", "rep", None),
            P(),
            P(),
            P(None, ("loop", "feat")),
        ),
        out_specs=(P(), P(), P("feat", "loop")),
        check_vma=False,
    )
```

time: 147 us -> 140 us (0.952)
  the two profiles are of different devices: /device:TPU:16 before, /device:TPU:1 now
where the time goes in v3:
time: 140 us; the launch traced here: 139 us
  Pallas kernels  137 us (98%)
  local copies, waits for them, and re-layouts  1.91 us (1%)
    pallas_call x1, Pallas kernels, shards(): pl.pallas_call(functools.partial(layers_kernel, (L, R, F), scale), out_sh...  133 us
    pallas_call x1, Pallas kernels, dense_sections(): pl.pallas_call(place_kernel, out_shape=jax.ShapeDtypeStruct((sections, ch...  3.47 us

profile of v3, /device:TPU:1, one launch (start us, length us, event | category | flops | bytes accessed | tf_op | source)
XLA Modules:
  0.0 139.1 jit_solution(2594195977431660652)
XLA Ops:
  0.6 0.0 copy-start.1
  0.6 0.0 copy-start.3
  0.7 0.0 copy-start.2
  0.7 0.0 copy-start
  0.7 3.5 %place_tiles.1.dense = bf16[8,4,1024,256]{3,2,1,0:T(8,128)(2,1)S(1)} custom-call(s32[1,1,2,112]{3,2,1,0:T(2,128)} %coords_hbm.1, s32[1,1,8]{2,1,0:T(1,128)} %counts_hbm.1, bf16[1,1,112,128,128]{4,3,2,1,0:T(8,128)(2,1)} %tiles_hbm.1), custom_call_target="tpu_custom_call" | custom-call | tf_op jit(solution)/shard_map/place_tiles/pallas_call | solution.py:52
  4.2 0.0 copy-done.1
  4.2 0.0 copy-done.3
  4.2 0.0 copy-done.2
  4.2 0.0 copy-done
  4.2 133.0 %layers.1 = (bf16[32,1024]{1,0:T(8,128)(2,1)S(1)}, f32[128,128]{1,0:T(8,128)S(1)}, f32[128,128]{1,0:T(8,128)S(1)}) custom-call(bf16[32,1024]{1,0:T(8,128)(2,1)S(1)} %copy-done, bf16[8,4,1024,256]{3,2,1,0:T(8,128)(2,1)S(1)} %place_tiles.1.dense, bf16[128,128]{1,0:T(8,128)(2,1)S(1)} %copy-done.2, bf16[128,128]{1,0:T(8,128)(2,1)S(1)} %copy-done.3, ...), custom_call_target="tpu_custom_call" | custom-call | tf_op jit(solution)/shard_map/layers/pallas_call | solution.py:512
  137.2 0.6 copy.13
  137.9 0.6 copy.14
  138.5 0.6 copy.15
Async XLA Ops:
  0.6 3.5 %copy-start.1 = (bf16[128,256]{1,0:T(8,128)(2,1)S(1)}, bf16[128,256]{1,0:T(8,128)(2,1)}, u32[]{:S(2)}) copy-start(bf16[128,256]{1,0:T(8,128)(2,1)} %cot_ref.1) | copy-start | bytes 196612
  0.6 3.5 %copy-start.3 = (bf16[128,128]{1,0:T(8,128)(2,1)S(1)}, bf16[128,128]{1,0:T(8,128)(2,1)}, u32[]{:S(2)}) copy-start(bf16[128,128]{1,0:T(8,128)(2,1)} %w2.1) | copy-start | bytes 98308
  0.7 3.5 %copy-start.2 = (bf16[128,128]{1,0:T(8,128)(2,1)S(1)}, bf16[128,128]{1,0:T(8,128)(2,1)}, u32[]{:S(2)}) copy-start(bf16[128,128]{1,0:T(8,128)(2,1)} %w1.1) | copy-start | bytes 98308
  0.7 3.5 %copy-start = (bf16[32,1024]{1,0:T(8,128)(2,1)S(1)}, bf16[32,1024]{1,0:T(8,128)(2,1)}, u32[]{:S(2)}) copy-start(bf16[32,1024]{1,0:T(8,128)(2,1)} %feat_ref.1) | copy-start | bytes 196612

commit v4 on v3

--- a/solution.py
+++ b/solution.py
@@ -121,9 +121,6 @@
 
     for m in range(1, S):
         greet(at_loop(i + m * R), r, f)
-    for b in range(F):
-        greet(at_loop(behind - R), r, b)
-        greet(at_loop(behind + R), r, b)
     for a in range(R):
         for b in range(F):
             if (a, b) != (0, 0):
@@ -149,22 +146,18 @@
                 ru[p, 1, q] = zero
     wt[0] = w1[...].T
     wt[1] = w2[...].T
-    pl.semaphore_wait(barrier, S - 1 + 2 * F + R * F - 1 + (R - 1) * F + jnp.where(r != 0, F + R * F, 0))
+    pl.semaphore_wait(barrier, S - 1 + R * F - 1 + (R - 1) * F + jnp.where(r != 0, F + R * F, 0))
 
     def to_ring(p, src, q, ssem, ff):
-        for n, (k, to) in enumerate(((1, at_loop(ahead + R)), (S - 1, at_loop(ahead - R)), (0, ahead))):
-            def away(n=n, k=k, to=to):
-                remote(src, hbuf.at[p, k, q], ssem.at[n], ringr.at[p, k, q], (to, r, ff)).start()
-
-            def here(k=k):
-                local(src, hbuf.at[p, k, q], ringr.at[p, k, q]).start()
-
-            if k:
-                away()
-            else:
-                mine = (r == 0) & (ff == f)
-                pl.when(mine)(here)
-                pl.when(jnp.logical_not(mine))(away)
+        mine = (r == 0) & (ff == f)
+
+        @pl.when(mine)
+        def _():
+            local(src, hbuf.at[p, 0, q], ringr.at[p, 0, q]).start()
+
+        @pl.when(jnp.logical_not(mine))
+        def _():
+            remote(src, hbuf.at[p, 0, q], ssem, ringr.at[p, 0, q], (ahead, r, ff)).start()
 
     for q in range(F):
         to_ring(0, feat_ref.at[:, pl.ds(q * C, C)], q, p0s.at[q], f)
@@ -179,22 +172,30 @@
         def term(k, q):
             return nt_dot(hbuf[p, k, q], dense[k, q])
 
+        def first(q, carry):
+            here(0, q)
+            hop(0, 1, q, fs.at[p, 0, q], up)
+            hop(0, S - 1, q, bs.at[p, 0, q], dn)
+            value = term(0, q)
+
+            @pl.when(q == 0)
+            def _():
+                acc[...] = value
+
+            @pl.when(q != 0)
+            def _():
+                acc[...] += value
+
+            return carry
+
+        lax.fori_loop(0, F, first, 0)
+
         def near(q, carry):
             here(1, q)
-            hop(1, 2, q, fs.at[p, 0, q], up)
+            hop(1, 2, q, fs.at[p, 1, q], up)
             here(S - 1, q)
-            hop(S - 1, S - 2, q, bs.at[p, 0, q], dn)
-            here(0, q)
-            value = term(0, q) + term(1, q) + term(S - 1, q)
-
-            @pl.when(q == 0)
-            def _():
-                acc[...] = value
-
-            @pl.when(q != 0)
-            def _():
-                acc[...] += value
-
+            hop(S - 1, S - 2, q, bs.at[p, 1, q], dn)
+            acc[...] += term(1, q) + term(S - 1, q)
             return carry
 
         lax.fori_loop(0, F, near, 0)
@@ -204,16 +205,16 @@
 
             @pl.when(q < half)
             def _():
-                hop(2, H, q, fs.at[p, 2, q], up2)
-
-            hop(2, 3, q, fs.at[p, 1, q], up)
+                hop(2, H, q, fs.at[p, 3, q], up2)
+
+            hop(2, 3, q, fs.at[p, 2, q], up)
             here(S - 2, q)
 
             @pl.when(q >= half)
             def _():
-                hop(S - 2, H, q, bs.at[p, 2, q], dn2)
-
-            hop(S - 2, S - 3, q, bs.at[p, 1, q], dn)
+                hop(S - 2, H, q, bs.at[p, 3, q], dn2)
+
+            hop(S - 2, S - 3, q, bs.at[p, 2, q], dn)
             acc[...] += term(2, q) + term(S - 2, q)
             return carry
 
@@ -422,42 +423,30 @@
     spread(2, nn_dot(w1[...], dz_one).astype(BF16), dmb.at[1], dmr.at[1])
     grad_start(1, nt_dot(mix[0], dz_one))
     transposed(1)
-    for a in range(R):
-        for q in range(F):
-            done(fin.at[a, q], xr.at[3, a, q])
+    one = pst.at[0, 0]
+
     for q in range(F):
-        total = fin[0, q].astype(F32)
-        for a in range(1, R):
-            total = total + fin[a, q].astype(F32)
-        out_ref[:, q * C:(q + 1) * C] = total.astype(BF16)
-
-    grad_end(0, g2_ref)
-    grad_end(1, g1_ref)
-
-    one = pst.at[0, 0]
-
-    for q in range(F):
-        for n in range(2):
-            done(one, p0s.at[q, n])
-            done(one, h0s.at[q, n])
-        pl.when(r != 0)(functools.partial(done, one, p0s.at[q, 2]))
-        pl.when(jnp.logical_not((r == 0) & (f == q)))(functools.partial(done, one, h0s.at[q, 2]))
+        pl.when(jnp.logical_not((r == 0) & (f == q)))(functools.partial(done, one, h0s.at[q]))
+
+        @pl.when(r != 0)
+        def _():
+            done(one, p0s.at[q])
 
     for p in range(2):
         def sent_chunk(n, carry):
             s, q = lax.div(n, F), lax.rem(n, F)
 
-            @pl.when((s < 2) | (q < half))
+            @pl.when((s < 3) | (q < half))
             def _():
                 done(one, fs.at[p, s, q])
 
-            @pl.when((s < 2) | (q >= half))
+            @pl.when((s < 3) | (q >= half))
             def _():
                 done(one, bs.at[p, s, q])
 
             return carry
 
-        lax.fori_loop(0, 3 * F, sent_chunk, 0)
+        lax.fori_loop(0, 4 * F, sent_chunk, 0)
 
         def sent_sum(n, carry):
             s, q = lax.div(n, F), lax.rem(n, F)
@@ -495,6 +484,18 @@
         pl.when(r != 0)(functools.partial(done, one, xs.at[3, 0, b]))
         pl.when(f != b)(functools.partial(done, one, ls.at[1, b]))
         pl.when(f != b)(functools.partial(done, one, ls.at[2, b]))
+
+    for a in range(R):
+        for q in range(F):
+            done(fin.at[a, q], xr.at[3, a, q])
+    for q in range(F):
+        total = fin[0, q].astype(F32)
+        for a in range(1, R):
+            total = total + fin[a, q].astype(F32)
+        out_ref[:, q * C:(q + 1) * C] = total.astype(BF16)
+
+    grad_end(0, g2_ref)
+    grad_end(1, g1_ref)
 
 
 def shards(features, tile_values, tile_coords, section_counts, weight_one, weight_two, cotangent):
@@ -539,8 +540,8 @@
             pltpu.VMEM((2, piece, D), F32),
             pltpu.VMEM((2, R, F, piece, D), F32),
             dma((2, R, F)), dma((2, R, F)), dma((2, S)), dma((2, S)), dma((2, R, F)), dma((2, R, F)),
-            dma((2, S, F)), dma((2, 3, F)), dma((2, 3, F)),
-            dma((4, R, F)), dma((4, R, F)), dma((3, F)), dma((2, F)), dma((F, 3)), dma((F, 3)),
+            dma((2, S, F)), dma((2, 4, F)), dma((2, 4, F)),
+            dma((4, R, F)), dma((4, R, F)), dma((3, F)), dma((2, F)), dma((F,)), dma((F,)),
             dma((2, H, F)), dma((2, H, F)), dma((2, H, F)), dma((2, H, F)),
         ],
         compiler_params=pltpu.CompilerParams(

time: 140 us -> 139 us (level)
  Pallas kernels: 137 us -> 134 us
    pallas_call x1, Pallas kernels: 133 us -> 131 us  [shards(): pl.pallas_call(functools.partial(layers_kernel, (L, R, F), scale), out_sh...]
where the time goes in v4:
time: 139 us; the launch traced here: 137 us
  Pallas kernels  134 us (96%)
  local copies, waits for them, and re-layouts  1.91 us (1%)
    pallas_call x1, Pallas kernels, shards(): pl.pallas_call(functools.partial(layers_kernel, (L, R, F), scale), out_sh...  131 us
    pallas_call x1, Pallas kernels, dense_sections(): pl.pallas_call(place_kernel, out_shape=jax.ShapeDtypeStruct((sections, ch...  3.55 us

profile of v4, /device:TPU:1, one launch (start us, length us, event | category | flops | bytes accessed | tf_op | source)
XLA Modules:
  0.0 137.0 jit_solution(153837165776159051)
XLA Ops:
  0.6 0.0 copy-start.1
  0.6 0.0 copy-start.3
  0.7 0.0 copy-start.2
  0.7 0.0 copy-start
  0.7 3.6 %place_tiles.1.dense = bf16[8,4,1024,256]{3,2,1,0:T(8,128)(2,1)S(1)} custom-call(s32[1,1,2,112]{3,2,1,0:T(2,128)} %coords_hbm.1, s32[1,1,8]{2,1,0:T(1,128)} %counts_hbm.1, bf16[1,1,112,128,128]{4,3,2,1,0:T(8,128)(2,1)} %tiles_hbm.1), custom_call_target="tpu_custom_call" | custom-call | tf_op jit(solution)/shard_map/place_tiles/pallas_call | solution.py:52
  4.2 0.0 copy-done.1
  4.2 0.0 copy-done.3
  4.3 0.0 copy-done.2
  4.3 0.0 copy-done
  4.3 130.8 %layers.1 = (bf16[32,1024]{1,0:T(8,128)(2,1)S(1)}, f32[128,128]{1,0:T(8,128)S(1)}, f32[128,128]{1,0:T(8,128)S(1)}) custom-call(bf16[32,1024]{1,0:T(8,128)(2,1)S(1)} %copy-done, bf16[8,4,1024,256]{3,2,1,0:T(8,128)(2,1)S(1)} %place_tiles.1.dense, bf16[128,128]{1,0:T(8,128)(2,1)S(1)} %copy-done.2, bf16[128,128]{1,0:T(8,128)(2,1)S(1)} %copy-done.3, ...), custom_call_target="tpu_custom_call" | custom-call | tf_op jit(solution)/shard_map/layers/pallas_call | solution.py:513
  135.1 0.6 copy.13
  135.8 0.6 copy.14
  136.4 0.6 copy.15
Async XLA Ops:
  0.6 3.6 %copy-start.1 = (bf16[128,256]{1,0:T(8,128)(2,1)S(1)}, bf16[128,256]{1,0:T(8,128)(2,1)}, u32[]{:S(2)}) copy-start(bf16[128,256]{1,0:T(8,128)(2,1)} %cot_ref.1) | copy-start | bytes 196612
  0.6 3.6 %copy-start.3 = (bf16[128,128]{1,0:T(8,128)(2,1)S(1)}, bf16[128,128]{1,0:T(8,128)(2,1)}, u32[]{:S(2)}) copy-start(bf16[128,128]{1,0:T(8,128)(2,1)} %w2.1) | copy-start | bytes 98308
  0.7 3.6 %copy-start.2 = (bf16[128,128]{1,0:T(8,128)(2,1)S(1)}, bf16[128,128]{1,0:T(8,128)(2,1)}, u32[]{:S(2)}) copy-start(bf16[128,128]{1,0:T(8,128)(2,1)} %w1.1) | copy-start | bytes 98308
  0.7 3.6 %copy-start = (bf16[32,1024]{1,0:T(8,128)(2,1)S(1)}, bf16[32,1024]{1,0:T(8,128)(2,1)}, u32[]{:S(2)}) copy-start(bf16[32,1024]{1,0:T(8,128)(2,1)} %feat_ref.1) | copy-start | bytes 196612
